TPU v7x, 32 devices: a whole 2x2x4 slice. The times are simulated.
32 devices in a mesh: isl: 4 (over x, core), fsdp: 8 (over z, y).
Axes of the slice: x: 2, y: 2, z: 4, core: 2. Of those that a mesh axis runs over, the one named last changes fastest.
Arguments:
- weights: float32 [3, 7168, 4096], P(None, 'fsdp', 'isl'), may hold values from -6 to 6
- momentum: float32 [3, 7168, 4096], P(None, 'fsdp', 'isl'), may hold values from -0.12 to 0.12
- first_moment: bfloat16 [4, 3, 7168, 4096], P('isl', None, 'fsdp'), may hold values from -0.00029945374 to 0.00029945374
- second_moment: bfloat16 [4, 3, 7168, 4096], P('isl', None, 'fsdp'), may hold values from 9.95351e-09 to 9.953976e-06
- inputs: bfloat16 [2, 256, 4096], P(None, ('isl', 'fsdp')), may hold values from -6 to 6
- targets: bfloat16 [2, 256, 4096], P(None, ('isl', 'fsdp')), may hold values from -6 to 6
- overflow_step: int32 [4, 8], P('isl', 'fsdp'), may hold values from 0 to 15
Outputs:
- new_weights: float32 [3, 7168, 4096], P(None, 'fsdp', 'isl')
- new_momentum: float32 [3, 7168, 4096], P(None, 'fsdp', 'isl')
Inputs may be any that keep to these rules, and one draw needn't show every extreme that they name: `overflow_step`: A device reports an overflow at inner step k when its value equals k; values of 2 or more report none.
All inputs are finite; a program needn't handle non-finite values.
Results may differ from a plain program's by a relative error of at most 0.004.
Values may be sent and summed in bfloat16 or wider, within the bound.
A program may use at most 320 MiB of HBM per device.

v0:
```python
import math

import jax
import jax.numpy as jnp
from jax import lax
from jax.sharding import PartitionSpec as P

D = 4096
FF = 7168


inner_rate = 0.02
beta_first = 0.9
beta_second = 0.95
epsilon = 1e-08
decay_rate = 0.1
outer_rate = 0.7
nesterov_coef = 0.9


def silu_parts(preact):
    sigmoid_value = jax.nn.sigmoid(preact)
    return (preact * sigmoid_value, sigmoid_value * (1.0 + preact * (1.0 - sigmoid_value)))


def contract_last(left_side, right_side):
    return lax.dot_general(
        left_side, right_side, (((1,), (1,)), ((), ())), preferred_element_type=jnp.float32
    )


def contract_first(left_side, right_side):
    return lax.dot_general(
        left_side, right_side, (((0,), (0,)), ((), ())), preferred_element_type=jnp.float32
    )


def body(weights, momentum, first_moment, second_moment, inputs, targets, overflow_step):
    island_count = lax.axis_size("isl")
    gathered = lax.all_gather(weights.astype(jnp.bfloat16), "isl", axis=2, tiled=True).astype(
        weights.dtype
    )
    current = gathered
    moment_one = first_moment[0].astype(jnp.float32)
    moment_two = second_moment[0].astype(jnp.float32)
    inner_count = inputs.shape[0]
    island_tokens = inputs.shape[1] * lax.axis_size("fsdp")
    for inner_step in range(inner_count):
        rounded = current.astype(jnp.bfloat16)
        local_inputs = inputs[inner_step]
        local_targets = targets[inner_step]
        every_input = lax.all_gather(local_inputs, "fsdp", axis=0, tiled=True)
        gate_pre = contract_last(every_input, rounded[0]) / math.sqrt(D)
        up_pre = contract_last(every_input, rounded[1]) / math.sqrt(D)
        activated, slope = silu_parts(gate_pre)
        hidden = (activated * up_pre).astype(jnp.bfloat16)
        partial_value = jnp.dot(hidden, rounded[2], preferred_element_type=jnp.float32)
        summed = lax.psum_scatter(partial_value, "fsdp", scatter_dimension=0, tiled=True)
        outputs = local_inputs.astype(jnp.float32) + summed / math.sqrt(FF)
        own_slopes = ((outputs - local_targets.astype(jnp.float32)) / island_tokens).astype(
            jnp.bfloat16
        )
        slopes = lax.all_gather(own_slopes, "fsdp", axis=0, tiled=True)
        hidden_slope = contract_last(slopes, rounded[2]) / math.sqrt(FF)
        gate_slope = (hidden_slope * up_pre * slope).astype(jnp.bfloat16)
        up_slope = (hidden_slope * activated).astype(jnp.bfloat16)
        grad_gate = contract_first(gate_slope, every_input) / math.sqrt(D)
        grad_up = contract_first(up_slope, every_input) / math.sqrt(D)
        grad_down = contract_first(hidden, slopes) / math.sqrt(FF)
        gradient = jnp.stack([grad_gate, grad_up, grad_down])
        overflow_count = lax.psum(jnp.sum((overflow_step == inner_step).astype(jnp.int32)), "fsdp")
        skipped = overflow_count > 0
        next_one = beta_first * moment_one + (1.0 - beta_first) * gradient
        next_two = beta_second * moment_two + (1.0 - beta_second) * gradient * gradient
        next_weights = current - inner_rate * (
            next_one / (jnp.sqrt(next_two) + epsilon) + decay_rate * current
        )
        current = jnp.where(skipped, current, next_weights)
        moment_one = jnp.where(skipped, moment_one, next_one)
        moment_two = jnp.where(skipped, moment_two, next_two)
    pseudo_term = gathered - current
    pseudo_sum = lax.psum_scatter(
        pseudo_term.astype(jnp.bfloat16), "isl", scatter_dimension=2, tiled=True
    ).astype(jnp.float32)
    outer_delta = pseudo_sum / island_count
    new_momentum = nesterov_coef * momentum + outer_delta
    new_weights = weights - outer_rate * (outer_delta + nesterov_coef * new_momentum)
    return (new_weights, new_momentum)


def solution(mesh):
    in_specs = (
        P(None, "fsdp", "isl"),
        P(None, "fsdp", "isl"),
        P("isl", None, "fsdp", None),
        P("isl", None, "fsdp", None),
        P(None, ("isl", "fsdp"), None),
        P(None, ("isl", "fsdp"), None),
        P("isl", "fsdp"),
    )
    out_specs = (P(None, "fsdp", "isl"), P(None, "fsdp", "isl"))
    return jax.shard_map(body, mesh=mesh, in_specs=in_specs, out_specs=out_specs, check_vma=False)
```

profile of v0, /device:TPU:0, one launch (start us, length us, event | category | flops | bytes accessed | tf_op | source)
XLA Modules:
  0.0 742.3 jit_solution(11448061210267699757)
XLA Ops:
  7.2 0.0 copy-start.1
  7.2 0.0 copy-start.2
  7.2 0.0 all-gather.4.cloned.1.call-start
  7.2 7.5 %convert_element_type.72 = bf16[3,896,1024]{2,1,0:T(8,128)(2,1)} convert(f32[3,896,1024]{2,1,0:T(8,128)} %param.7) | non-fusion elementwise | flops 2752512 | bytes 16515072 | tf_op jit(solution)/shard_map/convert_element_type | solution.py:40
  14.7 0.0 all-gather.4.cloned.1.call-update
  14.8 0.0 reduce-scatter.4.cloned.1.call-start
  14.8 0.0 copy-done.1
  14.8 33.0 %all-gather = bf16[1,64,4096]{2,1,0:T(8,128)(2,1)S(1)} all-gather(bf16[1,8,4096]{2,1,0:T(8,128)(2,1)S(1)} %get-tuple-element.7), channel_id=2, replica_groups=mesh['isl'=4,'fsdp'=8] {'fsdp'}, dimensions={1}, use_global_device_ids=true | all-gather | bytes 589824 | tf_op jit(solution)/shard_map/all_gather | solution.py:52
  47.9 107.2 %all-gather.4.cloned.1.call-done = bf16[3,896,4096]{2,1,0:T(8,128)(2,1)} async-done(((bf16[3,896,1024]{2,1,0:T(8,128)(2,1)}), bf16[3,896,4096]{2,1,0:T(8,128)(2,1)}) %all-gather.4.cloned.1.call-update) | async-done | bytes 22020112 | tf_op jit(solution)/shard_map/all_gather | solution.py:40
  155.0 5.4 fusion.24
  160.5 5.4 multiply_convert_fusion.5
  165.9 5.5 fusion.19
  171.4 0.0 reduce-scatter.4.cloned.1.call-update
  171.4 0.0 reduce-scatter.6.cloned.1.call-start
  172.1 13.0 %all-reduce = (s32[]{:T(128)}, s32[]{:T(128)}) all-reduce(s32[]{:T(128)} %bitcast.1, s32[]{:T(128)} %bitcast), channel_id=1, replica_groups=mesh['isl'=4,'fsdp'=8] {'fsdp'}, use_global_device_ids=true, to_apply=%region_1.0 | all-reduce | flops 2 | bytes 16 | tf_op jit(solution)/shard_map/psum | solution.py:71
  185.8 31.7 %all-gather.1 = bf16[1,64,4096]{2,1,0:T(8,128)(2,1)S(1)} all-gather(bf16[1,8,4096]{2,1,0:T(8,128)(2,1)S(1)} %get-tuple-element.6), channel_id=3, replica_groups=mesh['isl'=4,'fsdp'=8] {'fsdp'}, dimensions={1}, use_global_device_ids=true | all-gather | bytes 589824 | tf_op jit(solution)/shard_map/all_gather | solution.py:52
  217.4 18.9 %reduce-scatter.4.cloned.1.call-done = f32[8,4096]{1,0:T(8,128)} async-done(((f32[64,4096]{1,0:T(8,128)}), f32[8,4096]{1,0:T(8,128)}) %reduce-scatter.4.cloned.1.call-update) | async-done | bytes 131088 | tf_op jit(solution)/shard_map/reduce_scatter | solution.py:58
  236.4 0.0 copy-done.2
  236.4 0.9 fusion.43
  237.3 31.7 %all_gather.17 = bf16[64,4096]{1,0:T(8,128)(2,1)S(1)} all-gather(bf16[8,4096]{1,0:T(8,128)(2,1)S(1)} %fusion.43), channel_id=1, replica_groups=mesh['isl'=4,'fsdp'=8] {'fsdp'}, dimensions={0}, use_global_device_ids=true | all-gather | bytes 589824 | tf_op jit(solution)/shard_map/all_gather | solution.py:63
  268.9 2.1 multiply_bitcast_fusion.3
  271.0 0.0 copy-start
  271.1 10.6 %fusion.23 = f32[64,896]{1,0:T(8,128)S(1)} fusion(bf16[64,4096]{1,0:T(8,128)(2,1)S(1)} %all_gather.17, bf16[3,896,4096]{2,1,0:T(8,128)(2,1)} %all-gather.4.cloned.1.call-done), kind=kOutput, calls=%fused_computation.51 | convolution fusion | flops 469819392 | bytes 8093696 | tf_op jit(solution)/shard_map/dot_general | solution.py:27
  281.7 7.2 multiply_bitcast_fusion.4
  288.9 7.3 multiply_bitcast_fusion.5
  296.2 47.5 %fusion.52 = bf16[3,896,4096]{2,1,0:T(8,128)(2,1)} fusion(bf16[1,3,896,4096]{3,2,1,0:T(8,128)(2,1)} %param.10, f32[1,896,4096]{2,1,0:T(8,128)S(1)} %multiply_bitcast_fusion.3, f32[1,896,4096]{2,1,0:T(8,128)} %multiply_bitcast_fusion.4, f32[1,896,4096]{2,1,0:T(8,128)} %multiply_bitcast_fusion.5, bf16[1,3,896,4096]{3,2,1,0:T(8,128)(2,1)} %param.9, ...), kind=kLoop, calls=%fused_computation.90 | loop fusion | flops 220200960 | bytes 132120576 | tf_op jit(solution)/shard_map/convert_element_type | solution.py:49
  343.8 0.0 copy-done
  343.8 5.4 fusion.27
  349.2 5.4 multiply_convert_fusion.2
  354.7 5.5 fusion.21
  360.1 0.0 reduce-scatter.6.cloned.1.call-update
  360.1 0.0 reduce-scatter.8.cloned.1.call-start
  360.7 62.5 %reduce-scatter.6.cloned.1.call-done = f32[8,4096]{1,0:T(8,128)} async-done(((f32[64,4096]{1,0:T(8,128)}), f32[8,4096]{1,0:T(8,128)}) %reduce-scatter.6.cloned.1.call-update) | async-done | bytes 131088 | tf_op jit(solution)/shard_map/reduce_scatter | solution.py:58
  423.2 0.9 fusion.41
  424.2 31.7 %all_gather.19 = bf16[64,4096]{1,0:T(8,128)(2,1)S(1)} all-gather(bf16[8,4096]{1,0:T(8,128)(2,1)S(1)} %fusion.41), channel_id=1, replica_groups=mesh['isl'=4,'fsdp'=8] {'fsdp'}, dimensions={0}, use_global_device_ids=true | all-gather | bytes 589824 | tf_op jit(solution)/shard_map/all_gather | solution.py:63
  455.9 5.4 fusion.22
  461.3 7.3 multiply_bitcast_fusion
  468.6 7.2 multiply_bitcast_fusion.1
  475.8 7.3 multiply_bitcast_fusion.2
  483.1 77.6 %fusion.13 = bf16[3,896,4096]{2,1,0:T(8,128)(2,1)} fusion(bf16[3,896,4096]{2,1,0:T(8,128)(2,1)} %all-gather.4.cloned.1.call-done, f32[1,896,4096]{2,1,0:T(8,128)} %multiply_bitcast_fusion, f32[1,896,4096]{2,1,0:T(8,128)} %multiply_bitcast_fusion.1, f32[1,896,4096]{2,1,0:T(8,128)} %multiply_bitcast_fusion.2, f32[1,896,4096]{2,1,0:T(8,128)} %copy-done, ...), kind=kLoop, calls=%fused_computation.24 | loop fusion | flops 429391872 | bytes 176160768 | tf_op jit(solution)/shard_map/convert_element_type | solution.py:83
  560.7 0.0 reduce-scatter.8.cloned.1.call-update
  560.7 155.7 %reduce-scatter.8.cloned.1.call-done = bf16[3,896,1024]{2,1,0:T(8,128)(2,1)} async-done(((bf16[3,896,4096]{2,1,0:T(8,128)(2,1)}), bf16[3,896,1024]{2,1,0:T(8,128)(2,1)}) %reduce-scatter.8.cloned.1.call-update) | async-done | bytes 5505040 | tf_op jit(solution)/shard_map/reduce_scatter | solution.py:82
  716.4 19.4 %multiply_subtract_fusion = (f32[3,896,1024]{2,1,0:T(8,128)}, f32[3,896,1024]{2,1,0:T(8,128)}) fusion(f32[3,896,1024]{2,1,0:T(8,128)} %param.7, bf16[3,896,1024]{2,1,0:T(8,128)(2,1)} %reduce-scatter.8.cloned.1.call-done, f32[3,896,1024]{2,1,0:T(8,128)} %param.8), kind=kLoop, calls=%fused_computation.33 | loop fusion | flops 22020096 | bytes 49545216 | tf_op jit(solution)/shard_map/sub | solution.py:87
  (1 shorter events, 0.0 us)
Async XLA Ops:
  7.2 7.7 %copy-start.1 = (bf16[2,8,4096]{2,1,0:T(8,128)(2,1)S(1)}, bf16[2,8,4096]{2,1,0:T(8,128)(2,1)}, u32[]{:S(2)}) copy-start(bf16[2,8,4096]{2,1,0:T(8,128)(2,1)} %param.11) | copy-start | bytes 393220
  7.2 229.2 %copy-start.2 = (bf16[2,8,4096]{2,1,0:T(8,128)(2,1)S(1)}, bf16[2,8,4096]{2,1,0:T(8,128)(2,1)}, u32[]{:S(2)}) copy-start(bf16[2,8,4096]{2,1,0:T(8,128)(2,1)} %param.12) | copy-start | bytes 393220
  7.2 147.8 %all-gather.4.cloned.1.call-start = ((), (), s32[]{:S(2)}) async-start(), calls=%async_computation.3 | async-start | bytes 27525120 | tf_op jit(solution)/shard_map/all_gather | solution.py:40
  14.8 221.6 %reduce-scatter.4.cloned.1.call-start = ((), (), s32[]{:S(2)}) async-start(), calls=%async_computation.4 | async-start | bytes 1179648 | tf_op jit(solution)/shard_map/reduce_scatter | solution.py:58
  171.4 251.8 %reduce-scatter.6.cloned.1.call-start = ((), (), s32[]{:S(2)}) async-start(), calls=%async_computation.5 | async-start | bytes 1179648 | tf_op jit(solution)/shard_map/reduce_scatter | solution.py:58
  271.0 72.7 %copy-start = (f32[1,896,4096]{2,1,0:T(8,128)}, f32[1,896,4096]{2,1,0:T(8,128)S(1)}, u32[]{:S(2)}) copy-start(f32[1,896,4096]{2,1,0:T(8,128)S(1)} %multiply_bitcast_fusion.3) | copy-start | bytes 44040196
  360.1 356.3 %reduce-scatter.8.cloned.1.call-start = ((), (), s32[]{:S(2)}) async-start(), calls=%async_computation.6 | async-start | bytes 27525120 | tf_op jit(solution)/shard_map/reduce_scatter | solution.py:82
Sparse Core Ops, SparseCore 0:
  14.9 140.0 all-gather.3
  171.5 64.7 reduce-scatter.3
  360.3 62.9 reduce-scatter.5
  560.8 155.5 reduce-scatter.7
where the time goes:
time: 743 us; the launch traced here: 742 us
  waiting for transfers between devices  344 us (46%)
  other arithmetic  154 us (21%)
  blocking collectives  141 us (19%)
  matrix products  87.2 us (12%)
  between operations  15.7 us (2%)
    reduce_scatter x1, waiting for transfers between devices, body(): lax.psum_scatter(pseudo_term.astype(jnp.bfloat16), 'isl', scatter_dimensi...  156 us
    all_gather x1, waiting for transfers between devices, body(): lax.all_gather(weights.astype(jnp.bfloat16), 'isl', axis=2, tiled=True)  107 us
    reduce_scatter x2, waiting for transfers between devices, body(): lax.psum_scatter(partial_value, 'fsdp', scatter_dimension=0, tiled=True)  81.4 us
    convert_element_type x1, other arithmetic, body(): pseudo_term.astype(jnp.bfloat16)  77.6 us
    all_gather x2, blocking collectives, body(): every_input = lax.all_gather(local_inputs, 'fsdp', axis=0, tiled=True)  64.7 us
    all_gather x2, blocking collectives, body(): slopes = lax.all_gather(own_slopes, 'fsdp', axis=0, tiled=True)  63.4 us
    convert_element_type x1, other arithmetic, body(): rounded = current.astype(jnp.bfloat16)  47.5 us
    dot_general x6, matrix products, contract_first(): lax.dot_general(left_side, right_side, (((0,), (0,)), ((), ())), preferre...  38.4 us
  transfers between devices with their start and end apart: 4, of which 4 were waited for; matrix products, arithmetic and copies ran while one was open for 0% of the time, Pallas kernels for 0%

commit v1 on v0

v1 whole, which is shorter than its diff:
```python
import functools
import math

import jax
import jax.numpy as jnp
from jax import lax
from jax.experimental import pallas as pl
from jax.experimental.pallas import tpu as pltpu
from jax.sharding import PartitionSpec as P

MESH = pl.DeviceIdType.MESH

inner_rate = 0.02
beta_first = 0.9
beta_second = 0.95
epsilon = 1e-08
decay_rate = 0.1
outer_rate = 0.7
nesterov_coef = 0.9


def silu_parts(preact):
    sigmoid_value = jax.nn.sigmoid(preact)
    return (preact * sigmoid_value, sigmoid_value * (1.0 + preact * (1.0 - sigmoid_value)))


def contract_last(left_side, right_side):
    return lax.dot_general(
        left_side, right_side, (((1,), (1,)), ((), ())), preferred_element_type=jnp.float32
    )


def enter(peers):
    barrier = pltpu.get_barrier_semaphore()
    for peer in peers:
        pl.semaphore_signal(barrier, inc=1, device_id=peer, device_id_type=MESH)
    pl.semaphore_wait(barrier, len(peers))


def gather_kernel(n, n_isl, x_ref, flag_ref, out_ref, count_ref, got, flags, counts, own,
                  send_sem, recv_sem, fsend_sem, frecv_sem, csend_sem, crecv_sem):
    isl = lax.axis_index("isl")
    me = lax.axis_index("fsdp")
    enter(
        [{"fsdp": lax.rem(me + d, n)} for d in range(1, n)]
        + [{"isl": lax.rem(isl + d, n_isl)} for d in range(1, n_isl)]
    )
    copies = []
    for d in range(1, n):
        to = {"fsdp": lax.rem(me + d, n)}
        small = pltpu.make_async_remote_copy(
            flag_ref, flags.at[d - 1], fsend_sem.at[d - 1], frecv_sem.at[d - 1],
            device_id=to, device_id_type=MESH)
        small.start()
        big = pltpu.make_async_remote_copy(
            x_ref, got.at[d - 1], send_sem.at[d - 1], recv_sem.at[d - 1],
            device_id=to, device_id_type=MESH)
        big.start()
        copies.append((small, big))
    total = flag_ref[...]
    for d in range(1, n):
        copies[d - 1][0].wait()
        total = total + flags[d - 1]
    own[...] = total
    sent = []
    for d in range(1, n_isl):
        copy = pltpu.make_async_remote_copy(
            own, counts.at[d - 1], csend_sem.at[d - 1], crecv_sem.at[d - 1],
            device_id={"isl": lax.rem(isl + d, n_isl)}, device_id_type=MESH)
        copy.start()
        sent.append(copy)
    count_ref[0] = total
    for k in range(x_ref.shape[0]):
        out_ref[k, me] = x_ref[k]
    for d in range(1, n):
        copies[d - 1][1].wait()
        for k in range(x_ref.shape[0]):
            out_ref[k, lax.rem(me + n - d, n)] = got[d - 1, k]
    for d in range(1, n_isl):
        sent[d - 1].wait()
        count_ref[d] = counts[d - 1]


def gather_inputs(x, flags, n, n_isl):
    steps, rows, width = x.shape
    vmem = pl.BlockSpec(memory_space=pltpu.VMEM)
    return pl.pallas_call(
        functools.partial(gather_kernel, n, n_isl),
        out_shape=(jax.ShapeDtypeStruct((steps, n, rows, width), x.dtype),
                   jax.ShapeDtypeStruct((n_isl, 8, 128), jnp.float32)),
        in_specs=[vmem, vmem],
        out_specs=(vmem, vmem),
        scratch_shapes=[
            pltpu.VMEM((n - 1, steps, rows, width), x.dtype),
            pltpu.VMEM((n - 1, 8, 128), jnp.float32),
            pltpu.VMEM((n_isl - 1, 8, 128), jnp.float32),
            pltpu.VMEM((8, 128), jnp.float32),
            pltpu.SemaphoreType.DMA((n - 1,)),
            pltpu.SemaphoreType.DMA((n - 1,)),
            pltpu.SemaphoreType.DMA((n - 1,)),
            pltpu.SemaphoreType.DMA((n - 1,)),
            pltpu.SemaphoreType.DMA((n_isl - 1,)),
            pltpu.SemaphoreType.DMA((n_isl - 1,)),
        ],
        compiler_params=pltpu.CompilerParams(
            collective_id=0, has_side_effects=True, vmem_limit_bytes=40 << 20),
        name="gather_inputs",
    )(x, flags)


def slopes_kernel(n, scale, inverse, part_ref, x_ref, y_ref, out_ref, got, own, back,
                  send_sem, recv_sem, send_two, recv_two):
    me = lax.axis_index("fsdp")
    enter([{"fsdp": lax.rem(me + d, n)} for d in range(1, n)])
    copies = []
    for d in range(1, n):
        peer = lax.rem(me + d, n)
        copy = pltpu.make_async_remote_copy(
            part_ref.at[peer], got.at[d - 1], send_sem.at[d - 1], recv_sem.at[d - 1],
            device_id={"fsdp": peer}, device_id_type=MESH)
        copy.start()
        copies.append(copy)
    total = part_ref[me].astype(jnp.float32)
    for d in range(1, n):
        copies[d - 1].wait()
        total = total + got[d - 1].astype(jnp.float32)
    outputs = x_ref[...].astype(jnp.float32) + total * scale
    own[...] = ((outputs - y_ref[...].astype(jnp.float32)) * inverse).astype(jnp.bfloat16)
    copies = []
    for d in range(1, n):
        copy = pltpu.make_async_remote_copy(
            own, back.at[d - 1], send_two.at[d - 1], recv_two.at[d - 1],
            device_id={"fsdp": lax.rem(me + d, n)}, device_id_type=MESH)
        copy.start()
        copies.append(copy)
    out_ref[me] = own[...]
    for d in range(1, n):
        copies[d - 1].wait()
        out_ref[lax.rem(me + n - d, n)] = back[d - 1]


def island_slopes(part, x, y, hidden_units):
    n, rows, width = part.shape
    vmem = pl.BlockSpec(memory_space=pltpu.VMEM)
    return pl.pallas_call(
        functools.partial(
            slopes_kernel, n, 1.0 / math.sqrt(hidden_units), 1.0 / (n * rows)),
        out_shape=jax.ShapeDtypeStruct((n, rows, width), jnp.bfloat16),
        in_specs=[vmem] * 3,
        out_specs=vmem,
        scratch_shapes=[
            pltpu.VMEM((n - 1, rows, width), part.dtype),
            pltpu.VMEM((rows, width), jnp.bfloat16),
            pltpu.VMEM((n - 1, rows, width), jnp.bfloat16),
            pltpu.SemaphoreType.DMA((n - 1,)),
            pltpu.SemaphoreType.DMA((n - 1,)),
            pltpu.SemaphoreType.DMA((n - 1,)),
            pltpu.SemaphoreType.DMA((n - 1,)),
        ],
        compiler_params=pltpu.CompilerParams(
            collective_id=1, has_side_effects=True, vmem_limit_bytes=40 << 20),
        name="island_slopes",
    )(part, x, y)


def first_kernel(width, coef_ref, m_ref, v_ref, lhs_ref, rhs_ref, out_ref):
    k = pl.program_id(0)
    grad_m, grad_v = coef_ref[k, 0], coef_ref[k, 1]
    eps, factor = coef_ref[k, 2], coef_ref[k, 3]
    lhs = lhs_ref[0]
    for start in range(0, m_ref.shape[2], width):
        cols = pl.ds(start, width)
        grad = jnp.dot(lhs, rhs_ref[0, :, cols], preferred_element_type=jnp.float32)
        first = m_ref[0, :, cols].astype(jnp.float32) + grad_m * grad
        second = v_ref[0, :, cols].astype(jnp.float32) + grad_v * (grad * grad)
        root = second * lax.rsqrt(second) + eps
        out_ref[0, :, cols] = (factor * first / root).astype(jnp.bfloat16)


def first_update(coefs, m, v, lhs, rhs):
    mats, rows, width = m.shape
    tokens = lhs.shape[2]
    tile = next(t for t in (128, 64, 32, 16, 8) if rows % t == 0)
    block = pl.BlockSpec((1, tile, width), lambda k, r: (k, r, 0))
    return pl.pallas_call(
        functools.partial(first_kernel, min(256, width)),
        grid=(mats, rows // tile),
        out_shape=jax.ShapeDtypeStruct(m.shape, jnp.bfloat16),
        in_specs=[
            pl.BlockSpec(memory_space=pltpu.SMEM),
            block,
            block,
            pl.BlockSpec((1, tile, tokens), lambda k, r: (k, r, 0)),
            pl.BlockSpec((1, tokens, width), lambda k, r: (k // 2, 0, 0)),
        ],
        out_specs=block,
        compiler_params=pltpu.CompilerParams(
            dimension_semantics=("arbitrary", "arbitrary"), vmem_limit_bytes=40 << 20),
        name="first_update",
    )(coefs, m, v, lhs, rhs)


SLOTS = 8
LAG = 4


def last_kernel(chunks, per, tile, quarter, width, coef_ref, m_ref, v_ref, p_ref, lhs0_ref,
                lhs1_ref, rhs0_ref, rhs1_ref, w_ref, mom_ref, neww_ref, newm_ref,
                keep, send_a, recv_a, near, send_b, recv_b,
                sa_sem, ra_sem, sb_sem, rb_sem, credit_a, credit_b):
    t = pl.program_id(0)
    me = lax.axis_index("isl")
    side, core = me // 2, lax.rem(me, 2)
    partner = {"isl": side * 2 + lax.rem(core + 1, 2)}
    far = {"isl": lax.rem(side + 1, 2) * 2 + core}

    @pl.when(t == 0)
    def _():
        enter([partner, far])

    def copy_a(slot):
        return pltpu.make_async_remote_copy(
            send_a.at[slot], recv_a.at[slot], sa_sem.at[slot], ra_sem.at[slot],
            device_id=partner, device_id_type=MESH)

    def copy_b(slot):
        return pltpu.make_async_remote_copy(
            send_b.at[slot], recv_b.at[slot], sb_sem.at[slot], rb_sem.at[slot],
            device_id=far, device_id_type=MESH)

    @pl.when(t < chunks)
    def _():
        slot = lax.rem(t, SLOTS)

        @pl.when(t >= SLOTS)
        def _():
            copy_a(slot).wait_send()
            pl.semaphore_wait(credit_a, 1)

        k = t // per
        g0m, g1m = coef_ref[k, 0], coef_ref[k, 1]
        g0v, g1v = coef_ref[k, 2], coef_ref[k, 3]
        eps, factor, hold = coef_ref[k, 4], coef_ref[k, 5], coef_ref[k, 6]
        lhs0, lhs1 = lhs0_ref[0], lhs1_ref[0]
        for role in range(4):
            owner = lax.rem(side + role // 2, 2) * 2 + lax.rem(core + role % 2, 2)
            for start in range(0, quarter, width):
                cols = pl.ds(pl.multiple_of(owner * quarter + start, 128), width)
                g0 = jnp.dot(lhs0, rhs0_ref[0, :, cols], preferred_element_type=jnp.float32)
                g1 = jnp.dot(lhs1, rhs1_ref[0, :, cols], preferred_element_type=jnp.float32)
                first = m_ref[0, :, cols].astype(jnp.float32) + g0m * g0 + g1m * g1
                second = (v_ref[0, :, cols].astype(jnp.float32) + g0v * (g0 * g0)
                          + g1v * (g1 * g1))
                root = second * lax.rsqrt(second) + eps
                term = (hold * p_ref[0, :, cols].astype(jnp.float32)
                        + factor * first / root).astype(jnp.bfloat16)
                if role % 2 == 0:
                    keep[slot, role // 2, :, pl.ds(start, width)] = term
                else:
                    send_a[slot, role // 2, :, pl.ds(start, width)] = term
        copy_a(slot).start()

    @pl.when((t >= 1) & (t < chunks + 1))
    def _():
        chunk = t - 1
        slot = lax.rem(chunk, SLOTS)
        copy_a(slot).wait_recv()

        @pl.when(chunk >= SLOTS)
        def _():
            copy_b(slot).wait_send()
            pl.semaphore_wait(credit_b, 1)

        send_b[slot] = (keep[slot, 1].astype(jnp.float32)
                        + recv_a[slot, 1].astype(jnp.float32)).astype(jnp.bfloat16)
        copy_b(slot).start()
        near[slot] = keep[slot, 0].astype(jnp.float32) + recv_a[slot, 0].astype(jnp.float32)

        @pl.when(chunk + SLOTS < chunks)
        def _():
            pl.semaphore_signal(credit_a, inc=1, device_id=partner, device_id_type=MESH)

    @pl.when(t >= LAG)
    def _():
        chunk = t - LAG
        slot = lax.rem(chunk, SLOTS)
        copy_b(slot).wait_recv()
        weights = w_ref[0]
        delta = (near[slot] + recv_b[slot].astype(jnp.float32)) * 0.25 + coef_ref[0, 7] * weights
        momentum = nesterov_coef * mom_ref[0] + delta
        newm_ref[0] = momentum
        neww_ref[0] = weights - outer_rate * (delta + nesterov_coef * momentum)

        @pl.when(chunk + SLOTS < chunks)
        def _():
            pl.semaphore_signal(credit_b, inc=1, device_id=far, device_id_type=MESH)

    @pl.when(t == chunks + LAG - 1)
    def _():
        for chunk in range(max(chunks - SLOTS, 0), chunks):
            copy_a(chunk % SLOTS).wait_send()
            copy_b(chunk % SLOTS).wait_send()


def last_update(coefs, m, v, p, lhs0, lhs1, rhs0, rhs1, w, mom):
    mats, rows, width = m.shape
    quarter = w.shape[2]
    tokens = lhs0.shape[2]
    tile = next(t for t in (64, 32, 16, 8) if rows % t == 0)
    per = rows // tile
    chunks = mats * per

    def ahead(t):
        t = jnp.minimum(t, chunks - 1)
        return (t // per, lax.rem(t, per), 0)

    def behind(t):
        t = jnp.maximum(t - LAG, 0)
        return (t // per, lax.rem(t, per), 0)

    def side(t):
        return (jnp.minimum(t, chunks - 1) // per // 2, 0, 0)

    wide = pl.BlockSpec((1, tile, width), ahead)
    thin = pl.BlockSpec((1, tile, tokens), ahead)
    rhs = pl.BlockSpec((1, tokens, width), side)
    state = pl.BlockSpec((1, tile, quarter), behind)
    return pl.pallas_call(
        functools.partial(last_kernel, chunks, per, tile, quarter, min(256, quarter)),
        grid=(chunks + LAG,),
        out_shape=(jax.ShapeDtypeStruct(w.shape, jnp.float32),) * 2,
        in_specs=[pl.BlockSpec(memory_space=pltpu.SMEM), wide, wide, wide, thin, thin, rhs, rhs,
                  state, state],
        out_specs=(state, state),
        scratch_shapes=[
            pltpu.VMEM((SLOTS, 2, tile, quarter), jnp.bfloat16),
            pltpu.VMEM((SLOTS, 2, tile, quarter), jnp.bfloat16),
            pltpu.VMEM((SLOTS, 2, tile, quarter), jnp.bfloat16),
            pltpu.VMEM((SLOTS, tile, quarter), jnp.float32),
            pltpu.VMEM((SLOTS, tile, quarter), jnp.bfloat16),
            pltpu.VMEM((SLOTS, tile, quarter), jnp.bfloat16),
            pltpu.SemaphoreType.DMA((SLOTS,)),
            pltpu.SemaphoreType.DMA((SLOTS,)),
            pltpu.SemaphoreType.DMA((SLOTS,)),
            pltpu.SemaphoreType.DMA((SLOTS,)),
            pltpu.SemaphoreType.REGULAR,
            pltpu.SemaphoreType.REGULAR,
        ],
        compiler_params=pltpu.CompilerParams(
            collective_id=2, has_side_effects=True, dimension_semantics=("arbitrary",),
            vmem_limit_bytes=48 << 20),
        name="last_update",
    )(coefs, m, v, p, lhs0, lhs1, rhs0, rhs1, w, mom)


def backward(slopes, hidden, hidden_slope, up_pre, activated, slope):
    gate_slope = (hidden_slope * up_pre * slope).astype(jnp.bfloat16)
    up_slope = (hidden_slope * activated).astype(jnp.bfloat16)
    return jnp.stack([gate_slope.T, up_slope.T, hidden.T])


def body(n_isl, n_fsdp, weights, momentum, first_moment, second_moment, inputs, targets,
         overflow_step):
    moment_one = first_moment[0]
    moment_two = second_moment[0]
    rows = inputs.shape[1]
    width = inputs.shape[2]
    local_hidden = weights.shape[1]
    hidden_units = local_hidden * n_fsdp
    tokens = rows * n_fsdp
    scale_in, scale_out = 1.0 / math.sqrt(width), 1.0 / math.sqrt(hidden_units)

    gathered = lax.all_gather(weights.astype(jnp.bfloat16), "isl", axis=2, tiled=True)
    line = lax.broadcasted_iota(jnp.int32, (8, 128), 0)
    flags = (line == overflow_step[0, 0]).astype(jnp.float32)
    every, counts = gather_inputs(inputs, flags, n_fsdp, n_isl)
    every = every.reshape(2, tokens, width)

    active = (counts[:, :2, 0] < 0.5).astype(jnp.float32)
    act0, act1 = active[0, 0], active[0, 1]
    shrink = inner_rate * decay_rate
    weight_part = jnp.sum(
        shrink * (active[:, 0] + active[:, 1]) - shrink * shrink * active[:, 0] * active[:, 1]
    ) / n_isl
    keep0, keep1 = 1.0 - shrink * act0, 1.0 - shrink * act1
    scales = jnp.array([scale_in, scale_in, scale_out], jnp.float32)
    zeros = jnp.zeros((3,), jnp.float32)
    root_second = math.sqrt(beta_second)
    coefs0 = jnp.stack([
        (1 - beta_first) / beta_first * scales,
        (1 - beta_second) / beta_second * scales * scales,
        zeros + epsilon / root_second,
        zeros + inner_rate * beta_first / root_second * act0,
    ], axis=1)
    one = 1.0 + (beta_first - 1.0) * act0
    two = 1.0 + (beta_second - 1.0) * act0
    root_two = jnp.sqrt(beta_second * two)
    coefs1 = jnp.stack([
        act0 * (1 - beta_first) / one * scales,
        (1 - beta_first) / (beta_first * one) * scales,
        act0 * (1 - beta_second) / two * scales * scales,
        (1 - beta_second) / (beta_second * two) * scales * scales,
        zeros + epsilon / root_two,
        zeros + inner_rate * act1 * beta_first * one / root_two,
        zeros + keep1,
        zeros + weight_part,
    ], axis=1)

    both = every.reshape(2 * tokens, width)
    gate_all = contract_last(both, gathered[0])
    up_all = contract_last(both, gathered[1])

    def down(part):
        return part.astype(jnp.bfloat16).reshape(n_fsdp, rows, width)

    gate_pre, up_pre = gate_all[:tokens] * scale_in, up_all[:tokens] * scale_in
    activated, slope = silu_parts(gate_pre)
    hidden0 = (activated * up_pre).astype(jnp.bfloat16)
    part = jnp.dot(hidden0, gathered[2], preferred_element_type=jnp.float32)
    slopes0 = island_slopes(down(part), inputs[0], targets[0], hidden_units)
    slopes0 = slopes0.reshape(tokens, width)
    hidden_slope = contract_last(slopes0, gathered[2]) * scale_out
    lhs0 = backward(slopes0, hidden0, hidden_slope, up_pre, activated, slope)
    rhs0 = jnp.stack([every[0], slopes0])
    step0 = first_update(coefs0, moment_one, moment_two, lhs0, rhs0)

    gate_pre = (keep0 * gate_all[tokens:] - contract_last(every[1], step0[0])) * scale_in
    up_pre = (keep0 * up_all[tokens:] - contract_last(every[1], step0[1])) * scale_in
    activated, slope = silu_parts(gate_pre)
    hidden1 = (activated * up_pre).astype(jnp.bfloat16)
    part = (keep0 * jnp.dot(hidden1, gathered[2], preferred_element_type=jnp.float32)
            - jnp.dot(hidden1, step0[2], preferred_element_type=jnp.float32))
    slopes1 = island_slopes(down(part), inputs[1], targets[1], hidden_units)
    slopes1 = slopes1.reshape(tokens, width)
    hidden_slope = (keep0 * contract_last(slopes1, gathered[2])
                    - contract_last(slopes1, step0[2])) * scale_out
    lhs1 = backward(slopes1, hidden1, hidden_slope, up_pre, activated, slope)
    rhs1 = jnp.stack([every[1], slopes1])
    return last_update(coefs1, moment_one, moment_two, step0, lhs0, lhs1, rhs0, rhs1,
                       weights, momentum)


def solution(mesh):
    in_specs = (
        P(None, "fsdp", "isl"),
        P(None, "fsdp", "isl"),
        P("isl", None, "fsdp", None),
        P("isl", None, "fsdp", None),
        P(None, ("isl", "fsdp"), None),
        P(None, ("isl", "fsdp"), None),
        P("isl", "fsdp"),
    )
    out_specs = (P(None, "fsdp", "isl"), P(None, "fsdp", "isl"))
    fn = functools.partial(body, mesh.shape["isl"], mesh.shape["fsdp"])
    return jax.shard_map(fn, mesh=mesh, in_specs=in_specs, out_specs=out_specs, check_vma=False)
```

time: 743 us -> 449 us (0.60)
  Pallas kernels: 0 us -> 243 us
  waiting for transfers between devices: 344 us -> 106 us
  other arithmetic: 154 us -> 8.92 us
  blocking collectives: 141 us -> 0 us
  matrix products: 87.2 us -> 49.5 us
  local copies, waits for them, and re-layouts: 0.02 us -> 16.6 us
    pallas_call x0 -> x5, Pallas kernels: none -> 243 us  [the longest x1 127 us: last_update(): pl.pallas_call(functools.partial(last_kernel, chunks, per, tile, quarter,...]
    reduce_scatter x3 -> x0, waiting for transfers between devices: 237 us -> none  [the longest x1 156 us: body(): lax.psum_scatter(pseudo_term.astype(jnp.bfloat16), 'isl', scatter_dimensi...]
    all_gather x4 -> x0, blocking collectives: 128 us -> none  [the longest x2 64.7 us: body(): every_input = lax.all_gather(local_inputs, 'fsdp', axis=0, tiled=True)]
    convert_element_type x4 -> x3, other arithmetic: 127 us -> 0.17 us  [the longest x1 0.16 us: body(): hidden0 = (activated * up_pre).astype(jnp.bfloat16)]
    dot_general x8 -> x3, matrix products: 49.3 us -> 13.5 us  [the longest x1 4.5 us: body(): jnp.dot(hidden1, step0[2], preferred_element_type=jnp.float32)]
    sub x1 -> x0, other arithmetic: 19.4 us -> none  [body(): weights - outer_rate * (outer_delta + nesterov_coef * new_momentum)]
    unnamed x6 -> x16, local copies, waits for them, and re-layouts: 0.01 us -> 15.2 us
    psum x1 -> x0, blocking collectives: 13 us -> none  [body(): lax.psum(jnp.sum((overflow_step == inner_step).astype(jnp.int32)), 'fsdp')]
  transfers between devices with their start and end apart: 4 -> 1, of which waited for: 4 -> 1; matrix products, arithmetic and copies ran while one was open for 0% -> 0% of each run, Pallas kernels for 0% -> 6%
where the time goes in v1:
time: 449 us; the launch traced here: 445 us
  Pallas kernels  243 us (54%)
  waiting for transfers between devices  106 us (24%)
  matrix products  49.5 us (11%)
  between operations  20.9 us (5%)
  local copies, waits for them, and re-layouts  16.6 us (4%)
  other arithmetic  8.92 us (2%)
    pallas_call x1, Pallas kernels, last_update(): pl.pallas_call(functools.partial(last_kernel, chunks, per, tile, quarter,...  127 us
    all_gather x1, waiting for transfers between devices, body(): lax.all_gather(weights.astype(jnp.bfloat16), 'isl', axis=2, tiled=True)  106 us
    pallas_call x2, Pallas kernels, island_slopes(): pl.pallas_call(functools.partial(slopes_kernel, n, 1.0 / math.sqrt(hidden...  55.6 us
    dot_general x7, matrix products, contract_last(): lax.dot_general(left_side, right_side, (((1,), (1,)), ((), ())), preferre...  36.1 us
    pallas_call x1, Pallas kernels, first_update(): pl.pallas_call(functools.partial(first_kernel, min(256, width)), grid=(ma...  35.5 us
    pallas_call x1, Pallas kernels, gather_inputs(): pl.pallas_call(functools.partial(gather_kernel, n, n_isl), out_shape=(jax...  25.3 us
    unnamed x16, local copies, waits for them, and re-layouts  15.2 us
  transfers between devices with their start and end apart: 1, of which 1 were waited for; matrix products, arithmetic and copies ran while one was open for 0% of the time, Pallas kernels for 6%

profile of v1, /device:TPU:0, one launch (start us, length us, event | category | flops | bytes accessed | tf_op | source)
XLA Modules:
  0.0 445.3 jit_solution(2985848600605606981)
XLA Ops:
  7.2 0.0 copy-start.6
  7.2 0.0 copy-start.5
  7.2 0.0 copy-start.3
  7.2 0.0 copy-start.4
  7.2 0.0 copy-start
  7.2 0.0 copy-start.2
  7.2 0.0 all-gather.2.cloned.1.call-start
  7.3 7.5 %convert_element_type.39 = bf16[3,896,1024]{2,1,0:T(8,128)(2,1)} convert(f32[3,896,1024]{2,1,0:T(8,128)} %w_ref.1) | non-fusion elementwise | flops 2752512 | bytes 16515072 | tf_op jit(solution)/shard_map/convert_element_type | solution.py:373
  14.8 0.0 all-gather.2.cloned.1.call-update
  15.5 0.1 iota.7.flag_ref
  15.5 0.0 copy-done
  15.5 25.3 %gather_inputs.1 = (bf16[2,8,8,4096]{3,2,1,0:T(8,128)(2,1)S(1)}, f32[4,8,128]{2,1,0:T(8,128)S(1)}) custom-call(bf16[2,8,4096]{2,1,0:T(8,128)(2,1)S(1)} %copy-done, f32[8,128]{1,0:T(8,128)S(1)} %iota.7.flag_ref), custom_call_target="tpu_custom_call" | custom-call | tf_op jit(solution)/shard_map/gather_inputs/pallas_call | solution.py:87
  40.9 0.1 copy.25
  41.0 0.5 fusion.40
  46.8 0.1 pad.12.clone
  46.9 0.1 pad.13.clone
  47.0 0.0 copy-done.6
  47.0 0.1 copy.29
  47.1 0.0 copy-done.5
  47.1 0.1 copy.27
  47.2 0.1 copy.28
  47.3 0.1 copy.26
  47.4 0.6 fusion.39
  48.7 0.1 stack.77.coef_ref
  48.8 0.0 copy-done.3
  48.8 0.0 copy-done.4
  48.8 0.1 maximum_maximum_fusion.coef_ref
  48.9 0.0 copy-done.2
  48.9 0.1 slice_bitcast_fusion.45
  49.0 106.2 %all-gather.2.cloned.1.call-done = bf16[3,896,4096]{2,1,0:T(8,128)(2,1)} async-done(((bf16[3,896,1024]{2,1,0:T(8,128)(2,1)}), bf16[3,896,4096]{2,1,0:T(8,128)(2,1)}) %all-gather.2.cloned.1.call-update) | async-done | bytes 22020112 | tf_op jit(solution)/shard_map/all_gather | solution.py:373
  155.2 5.1 %fusion.2 = f32[128,896]{0,1:T(8,128)S(1)} fusion(bf16[128,4096]{1,0:T(8,128)(2,1)S(1)} %bitcast.166, bf16[3,896,4096]{2,1,0:T(8,128)(2,1)} %all-gather.2.cloned.1.call-done), kind=kOutput, calls=%fused_computation.7 | convolution fusion | flops 939524096 | bytes 8847360 | tf_op jit(solution)/shard_map/dot_general | solution.py:28
  160.4 5.1 %fusion.3 = f32[128,896]{0,1:T(8,128)S(1)} fusion(bf16[128,4096]{1,0:T(8,128)(2,1)S(1)} %bitcast.167, bf16[3,896,4096]{2,1,0:T(8,128)(2,1)} %all-gather.2.cloned.1.call-done), kind=kOutput, calls=%fused_computation.9 | convolution fusion | flops 939524096 | bytes 8847360 | tf_op jit(solution)/shard_map/dot_general | solution.py:28
  165.5 0.2 multiply_convert_fusion.5
  165.7 4.5 %fusion.14.part_ref = bf16[8,8,4096]{2,1,0:T(8,128)(2,1)S(1)} fusion(bf16[64,896]{0,1:T(8,128)(2,1)S(1)} %multiply_convert_fusion.5, bf16[3,896,4096]{2,1,0:T(8,128)(2,1)} %all-gather.2.cloned.1.call-done), kind=kOutput, calls=%fused_computation.20 | convolution fusion | flops 470024192 | bytes 7979008 | tf_op jit(solution)/shard_map/dot_general | solution.py:419
  170.2 25.9 %island_slopes.2 = bf16[8,8,4096]{2,1,0:T(8,128)(2,1)S(1)} custom-call(bf16[8,8,4096]{2,1,0:T(8,128)(2,1)S(1)} %fusion.14.part_ref, bf16[8,4096]{1,0:T(8,128)(2,1)S(1)} %get-tuple-element.24.x_ref, bf16[8,4096]{1,0:T(8,128)(2,1)S(1)} %get-tuple-element.13.y_ref), custom_call_target="tpu_custom_call" | custom-call | tf_op jit(solution)/shard_map/island_slopes/pallas_call | solution.py:145
  196.1 0.1 pad_maximum_fusion.rhs_ref.rhs0_ref
  196.2 5.2 %fusion.36 = (bf16[1,896,64]{2,1,0:T(8,128)(2,1)S(1)}, bf16[1,896,64]{2,1,0:T(8,128)(2,1)S(1)}) fusion(f32[128,896]{0,1:T(8,128)S(1)} %fusion.3, f32[128,896]{0,1:T(8,128)S(1)} %fusion.2, bf16[3,896,4096]{2,1,0:T(8,128)(2,1)} %all-gather.2.cloned.1.call-done, bf16[8,8,4096]{2,1,0:T(8,128)(2,1)S(1)} %island_slopes.2), kind=kOutput, calls=%fused_computation.60 | convolution fusion | flops 470679552 | bytes 8552448 | tf_op jit(solution)/shard_map/dot_general | solution.py:28
  201.4 0.2 pad_maximum_fusion.2.lhs_ref.lhs0_ref
  201.6 35.5 %first_update.1.p_ref = bf16[3,896,4096]{2,1,0:T(8,128)(2,1)} custom-call(f32[3,4]{1,0:T(4,128)S(1)} %maximum_maximum_fusion.coef_ref, bf16[3,896,4096]{2,1,0:T(8,128)(2,1)} %bitcast.168, bf16[3,896,4096]{2,1,0:T(8,128)(2,1)} %bitcast.170, bf16[3,896,64]{2,1,0:T(8,128)(2,1)S(1)} %pad_maximum_fusion.2.lhs_ref.lhs0_ref, ...), custom_call_target="tpu_custom_call" | custom-call | tf_op jit(solution)/shard_map/first_update/pallas_call | solution.py:185
  237.1 5.1 %fusion.22 = f32[64,896]{0,1:T(8,128)S(1)} fusion(bf16[3,896,4096]{2,1,0:T(8,128)(2,1)} %first_update.1.p_ref, f32[128,896]{0,1:T(8,128)S(1)} %fusion.3, bf16[2,8,8,4096]{3,2,1,0:T(8,128)(2,1)S(1)} %get-tuple-element.5, f32[]{:T(128)} %bitcast.34), kind=kOutput, calls=%fused_computation.28 | convolution fusion | flops 469934080 | bytes 8552960 | tf_op jit(solution)/shard_map/dot_general | solution.py:28
  242.2 5.1 %multiply_convert_fusion.2 = (bf16[64,896]{0,1:T(8,128)(2,1)S(1)}, f32[64,896]{0,1:T(8,128)S(1)}) fusion(f32[64,896]{0,1:T(8,128)S(1)} %fusion.22, bf16[3,896,4096]{2,1,0:T(8,128)(2,1)} %first_update.1.p_ref, bf16[2,8,8,4096]{3,2,1,0:T(8,128)(2,1)S(1)} %get-tuple-element.5, f32[128,896]{0,1:T(8,128)S(1)} %fusion.2, f32[]{:T(128)} %bitcast.34), kind=kOutput, calls=%fused_computation.46 | convolution fusion | flops 470278144 | bytes 9126400 | tf_op jit(solution)/shard_map/dot_general | solution.py:28
  247.4 4.5 %fusion.10 = f32[64,4096]{1,0:T(8,128)S(1)} fusion(bf16[64,896]{0,1:T(8,128)(2,1)S(1)} %get-tuple-element.22, bf16[3,896,4096]{2,1,0:T(8,128)(2,1)} %all-gather.2.cloned.1.call-done, f32[]{:T(128)} %bitcast.34), kind=kOutput, calls=%fused_computation.16 | convolution fusion | flops 470024192 | bytes 8503808 | tf_op jit(solution)/shard_map/dot_general | solution.py:431
  251.9 4.5 %fusion.15.part_ref = bf16[8,8,4096]{2,1,0:T(8,128)(2,1)S(1)} fusion(f32[64,4096]{1,0:T(8,128)S(1)} %fusion.10, bf16[64,896]{0,1:T(8,128)(2,1)S(1)} %get-tuple-element.22, bf16[3,896,4096]{2,1,0:T(8,128)(2,1)} %first_update.1.p_ref), kind=kOutput, calls=%fused_computation.21 | convolution fusion | flops 470286336 | bytes 9027584 | tf_op jit(solution)/shard_map/dot_general | solution.py:432
  256.4 29.7 %island_slopes.3 = bf16[8,8,4096]{2,1,0:T(8,128)(2,1)S(1)} custom-call(bf16[8,8,4096]{2,1,0:T(8,128)(2,1)S(1)} %fusion.15.part_ref, bf16[8,4096]{1,0:T(8,128)(2,1)S(1)} %get-tuple-element.25.x_ref, bf16[8,4096]{1,0:T(8,128)(2,1)S(1)} %get-tuple-element.12.y_ref), custom_call_target="tpu_custom_call" | custom-call | tf_op jit(solution)/shard_map/island_slopes/pallas_call | solution.py:145
  286.1 5.1 %fusion.17 = f32[64,896]{0,1:T(8,128)S(1)} fusion(bf16[3,896,4096]{2,1,0:T(8,128)(2,1)} %all-gather.2.cloned.1.call-done, bf16[8,8,4096]{2,1,0:T(8,128)(2,1)S(1)} %island_slopes.3, f32[]{:T(128)} %bitcast.34), kind=kOutput, calls=%fused_computation.23 | convolution fusion | flops 469819392 | bytes 8094208 | tf_op jit(solution)/shard_map/dot_general | solution.py:28
  291.3 5.2 %fusion.35 = (bf16[1,896,64]{2,1,0:T(8,128)(2,1)S(1)}, bf16[1,896,64]{2,1,0:T(8,128)(2,1)S(1)}) fusion(f32[64,896]{0,1:T(8,128)S(1)} %fusion.22, f32[64,896]{0,1:T(8,128)S(1)} %get-tuple-element.23, f32[64,896]{0,1:T(8,128)S(1)} %fusion.17, bf16[3,896,4096]{2,1,0:T(8,128)(2,1)} %first_update.1.p_ref, bf16[8,8,4096]{2,1,0:T(8,128)(2,1)S(1)} %island_slopes.3), kind=kOutput, calls=%fused_computation.59 | convolution fusion | flops 470622208 | bytes 8781824 | tf_op jit(solution)/shard_map/dot_general | solution.py:28
  296.5 0.1 pad_maximum_fusion.1.rhs1_ref
  296.6 0.2 pad_maximum_fusion.3.lhs1_ref
  296.7 126.5 %last_update.1 = (f32[3,896,1024]{2,1,0:T(8,128)}, f32[3,896,1024]{2,1,0:T(8,128)}) custom-call(f32[3,8]{1,0:T(4,128)S(1)} %stack.77.coef_ref, bf16[3,896,4096]{2,1,0:T(8,128)(2,1)} %bitcast.169, bf16[3,896,4096]{2,1,0:T(8,128)(2,1)} %bitcast.171, bf16[3,896,4096]{2,1,0:T(8,128)(2,1)} %first_update.1.p_ref, ...), custom_call_target="tpu_custom_call" | custom-call | tf_op jit(solution)/shard_map/last_update/pallas_call | solution.py:328
  423.3 0.0 copy-start.1
  423.3 10.9 %copy.53 = f32[3,896,1024]{2,1,0:T(8,128)} copy(f32[3,896,1024]{2,1,0:T(8,128)} %get-tuple-element.28) | data formatting | bytes 22020096
  434.2 0.0 copy-done.1
  434.2 4.3 copy.54
  (9 shorter events, 0.1 us)
Async XLA Ops:
  7.2 39.8 %copy-start.6 = (f32[3]{0:T(128)S(1)}, f32[3]{0:T(128)}, u32[]{:S(2)}) copy-start(f32[3]{0:T(128)} %constant.70) | copy-start | bytes 40
  7.2 39.9 %copy-start.5 = (f32[3]{0:T(128)S(1)}, f32[3]{0:T(128)}, u32[]{:S(2)}) copy-start(f32[3]{0:T(128)} %constant.64.clone) | copy-start | bytes 40
  7.2 41.6 %copy-start.3 = (f32[3,1]{1,0:T(4,128)S(1)}, f32[3,1]{1,0:T(4,128)}, u32[]{:S(2)}) copy-start(f32[3,1]{1,0:T(4,128)} %constant.74) | copy-start | bytes 40
  7.2 41.6 %copy-start.4 = (f32[3,1]{1,0:T(4,128)S(1)}, f32[3,1]{1,0:T(4,128)}, u32[]{:S(2)}) copy-start(f32[3,1]{1,0:T(4,128)} %constant.72) | copy-start | bytes 40
  7.2 8.3 %copy-start = (bf16[2,8,4096]{2,1,0:T(8,128)(2,1)S(1)}, bf16[2,8,4096]{2,1,0:T(8,128)(2,1)}, u32[]{:S(2)}) copy-start(bf16[2,8,4096]{2,1,0:T(8,128)(2,1)} %x_ref.1) | copy-start | bytes 393220
  7.2 41.7 %copy-start.2 = (bf16[2,8,4096]{2,1,0:T(8,128)(2,1)S(1)}, bf16[2,8,4096]{2,1,0:T(8,128)(2,1)}, u32[]{:S(2)}) copy-start(bf16[2,8,4096]{2,1,0:T(8,128)(2,1)} %param.13) | copy-start | bytes 393220
  7.2 148.0 %all-gather.2.cloned.1.call-start = ((), (), s32[]{:S(2)}) async-start(), calls=%async_computation | async-start | bytes 27525120 | tf_op jit(solution)/shard_map/all_gather | solution.py:373
  423.3 10.9 %copy-start.1 = (f32[3,896,1024]{2,1,0:T(8,128)S(1)}, f32[3,896,1024]{2,1,0:T(8,128)}, u32[]{:S(2)}) copy-start(f32[3,896,1024]{2,1,0:T(8,128)} %get-tuple-element.29) | copy-start | bytes 33030148
Sparse Core Ops, SparseCore 0:
  14.9 140.2 all-gather.1

commit v2 on v1

--- a/solution.py
+++ b/solution.py
@@ -108,6 +108,86 @@
     )(x, flags)
 
 
+def preact_kernel(x_ref, w_ref, out_ref, w_half, got, keep, send_a, recv_a, send_b, recv_b,
+                  sx_sem, rx_sem, sa_sem, ra_sem, sb_sem, rb_sem):
+    me = lax.axis_index("isl")
+    side, core = me // 2, lax.rem(me, 2)
+    index = [lax.rem(side + r // 2, 2) * 2 + lax.rem(core + r % 2, 2) for r in range(4)]
+    enter([{"isl": index[r]} for r in (1, 2, 3)])
+    moved = {}
+    for r in (3, 2, 1):
+        moved[r] = pltpu.make_async_remote_copy(
+            x_ref.at[index[r]], got.at[r - 1], sx_sem.at[r - 1], rx_sem.at[r - 1],
+            device_id={"isl": index[r]}, device_id_type=MESH)
+        moved[r].start()
+    for half in range(2):
+        w_half[half] = w_ref[half].astype(jnp.bfloat16)
+
+    def copy_a(slot):
+        return pltpu.make_async_remote_copy(
+            send_a.at[slot], recv_a.at[slot], sa_sem.at[slot], ra_sem.at[slot],
+            device_id={"isl": index[1]}, device_id_type=MESH)
+
+    def partial(x):
+        return [contract_last(x, w_half[half]) for half in range(2)]
+
+    for half, value in enumerate(partial(x_ref[me])):
+        out_ref[half] = value
+    moved[1].wait()
+    for half, value in enumerate(partial(got[0])):
+        send_a[0, half] = value.astype(jnp.bfloat16)
+    copy_a(0).start()
+    moved[3].wait()
+    for half, value in enumerate(partial(got[2])):
+        send_a[1, half] = value.astype(jnp.bfloat16)
+    copy_a(1).start()
+    moved[2].wait()
+    for half, value in enumerate(partial(got[1])):
+        keep[half] = value
+    copy_a(1).wait()
+    for half in range(2):
+        send_b[half] = (keep[half] + recv_a[1, half].astype(jnp.float32)).astype(jnp.bfloat16)
+    last = pltpu.make_async_remote_copy(
+        send_b, recv_b, sb_sem, rb_sem, device_id={"isl": index[2]}, device_id_type=MESH)
+    last.start()
+    copy_a(0).wait()
+    for half in range(2):
+        out_ref[half] = out_ref[half] + recv_a[0, half].astype(jnp.float32)
+    last.wait()
+    for half in range(2):
+        out_ref[half] = out_ref[half] + recv_b[half].astype(jnp.float32)
+
+
+def preactivations(x, w):
+    n_isl, tokens, quarter = x.shape
+    rows = w.shape[1]
+    vmem = pl.BlockSpec(memory_space=pltpu.VMEM)
+    dma = pltpu.SemaphoreType.DMA
+    return pl.pallas_call(
+        preact_kernel,
+        grid=(1,),
+        out_shape=jax.ShapeDtypeStruct((2, tokens, rows), jnp.float32),
+        in_specs=[pl.BlockSpec((n_isl, tokens, quarter), lambda i: (0, 0, 0)),
+                  pl.BlockSpec((2, rows, quarter), lambda i: (0, 0, 0),
+                               pipeline_mode=pl.Buffered(1))],
+        out_specs=pl.BlockSpec((2, tokens, rows), lambda i: (0, 0, 0)),
+        scratch_shapes=[
+            pltpu.VMEM((2, rows, quarter), jnp.bfloat16),
+            pltpu.VMEM((3, tokens, quarter), jnp.bfloat16),
+            pltpu.VMEM((2, tokens, rows), jnp.float32),
+            pltpu.VMEM((2, 2, tokens, rows), jnp.bfloat16),
+            pltpu.VMEM((2, 2, tokens, rows), jnp.bfloat16),
+            pltpu.VMEM((2, tokens, rows), jnp.bfloat16),
+            pltpu.VMEM((2, tokens, rows), jnp.bfloat16),
+            dma((3,)), dma((3,)), dma((2,)), dma((2,)), dma, dma,
+        ],
+        compiler_params=pltpu.CompilerParams(
+            collective_id=3, has_side_effects=True, dimension_semantics=("arbitrary",),
+            vmem_limit_bytes=48 << 20),
+        name="preactivations",
+    )(x, w)
+
+
 def slopes_kernel(n, scale, inverse, part_ref, x_ref, y_ref, out_ref, got, own, back,
                   send_sem, recv_sem, send_two, recv_two):
     me = lax.axis_index("fsdp")
@@ -163,21 +243,25 @@
     )(part, x, y)
 
 
-def first_kernel(width, coef_ref, m_ref, v_ref, lhs_ref, rhs_ref, out_ref):
+def first_kernel(width, coef_ref, m_ref, v_ref, lhs_ref, rhs_ref, next_ref, out_ref, pre_ref):
     k = pl.program_id(0)
     grad_m, grad_v = coef_ref[k, 0], coef_ref[k, 1]
     eps, factor = coef_ref[k, 2], coef_ref[k, 3]
     lhs = lhs_ref[0]
+    total = jnp.zeros(pre_ref.shape[1:], jnp.float32)
     for start in range(0, m_ref.shape[2], width):
         cols = pl.ds(start, width)
         grad = jnp.dot(lhs, rhs_ref[0, :, cols], preferred_element_type=jnp.float32)
         first = m_ref[0, :, cols].astype(jnp.float32) + grad_m * grad
         second = v_ref[0, :, cols].astype(jnp.float32) + grad_v * (grad * grad)
         root = second * lax.rsqrt(second) + eps
-        out_ref[0, :, cols] = (factor * first / root).astype(jnp.bfloat16)
-
-
-def first_update(coefs, m, v, lhs, rhs):
+        term = (factor * first / root).astype(jnp.bfloat16)
+        out_ref[0, :, cols] = term
+        total = total + contract_last(term, next_ref[:, cols])
+    pre_ref[0] = total
+
+
+def first_update(coefs, m, v, lhs, rhs, following):
     mats, rows, width = m.shape
     tokens = lhs.shape[2]
     tile = next(t for t in (128, 64, 32, 16, 8) if rows % t == 0)
@@ -185,19 +269,21 @@
     return pl.pallas_call(
         functools.partial(first_kernel, min(256, width)),
         grid=(mats, rows // tile),
-        out_shape=jax.ShapeDtypeStruct(m.shape, jnp.bfloat16),
+        out_shape=(jax.ShapeDtypeStruct(m.shape, jnp.bfloat16),
+                   jax.ShapeDtypeStruct(lhs.shape, jnp.float32)),
         in_specs=[
             pl.BlockSpec(memory_space=pltpu.SMEM),
             block,
             block,
             pl.BlockSpec((1, tile, tokens), lambda k, r: (k, r, 0)),
             pl.BlockSpec((1, tokens, width), lambda k, r: (k // 2, 0, 0)),
+            pl.BlockSpec((tokens, width), lambda k, r: (0, 0)),
         ],
-        out_specs=block,
+        out_specs=(block, pl.BlockSpec((1, tile, tokens), lambda k, r: (k, r, 0))),
         compiler_params=pltpu.CompilerParams(
             dimension_semantics=("arbitrary", "arbitrary"), vmem_limit_bytes=40 << 20),
         name="first_update",
-    )(coefs, m, v, lhs, rhs)
+    )(coefs, m, v, lhs, rhs, following)
 
 
 SLOTS = 8
@@ -370,7 +456,7 @@
     tokens = rows * n_fsdp
     scale_in, scale_out = 1.0 / math.sqrt(width), 1.0 / math.sqrt(hidden_units)
 
-    gathered = lax.all_gather(weights.astype(jnp.bfloat16), "isl", axis=2, tiled=True)
+    down_weights = lax.all_gather(weights[2].astype(jnp.bfloat16), "isl", axis=1, tiled=True)
     line = lax.broadcasted_iota(jnp.int32, (8, 128), 0)
     flags = (line == overflow_step[0, 0]).astype(jnp.float32)
     every, counts = gather_inputs(inputs, flags, n_fsdp, n_isl)
@@ -407,8 +493,8 @@
     ], axis=1)
 
     both = every.reshape(2 * tokens, width)
-    gate_all = contract_last(both, gathered[0])
-    up_all = contract_last(both, gathered[1])
+    by_owner = both.reshape(2 * tokens, n_isl, width // n_isl).transpose(1, 0, 2)
+    gate_all, up_all = preactivations(by_owner, weights)
 
     def down(part):
         return part.astype(jnp.bfloat16).reshape(n_fsdp, rows, width)
@@ -416,23 +502,23 @@
     gate_pre, up_pre = gate_all[:tokens] * scale_in, up_all[:tokens] * scale_in
     activated, slope = silu_parts(gate_pre)
     hidden0 = (activated * up_pre).astype(jnp.bfloat16)
-    part = jnp.dot(hidden0, gathered[2], preferred_element_type=jnp.float32)
+    part = jnp.dot(hidden0, down_weights, preferred_element_type=jnp.float32)
     slopes0 = island_slopes(down(part), inputs[0], targets[0], hidden_units)
     slopes0 = slopes0.reshape(tokens, width)
-    hidden_slope = contract_last(slopes0, gathered[2]) * scale_out
+    hidden_slope = contract_last(slopes0, down_weights) * scale_out
     lhs0 = backward(slopes0, hidden0, hidden_slope, up_pre, activated, slope)
     rhs0 = jnp.stack([every[0], slopes0])
-    step0 = first_update(coefs0, moment_one, moment_two, lhs0, rhs0)
-
-    gate_pre = (keep0 * gate_all[tokens:] - contract_last(every[1], step0[0])) * scale_in
-    up_pre = (keep0 * up_all[tokens:] - contract_last(every[1], step0[1])) * scale_in
+    step0, moved = first_update(coefs0, moment_one, moment_two, lhs0, rhs0, every[1])
+
+    gate_pre = (keep0 * gate_all[tokens:] - moved[0].T) * scale_in
+    up_pre = (keep0 * up_all[tokens:] - moved[1].T) * scale_in
     activated, slope = silu_parts(gate_pre)
     hidden1 = (activated * up_pre).astype(jnp.bfloat16)
-    part = (keep0 * jnp.dot(hidden1, gathered[2], preferred_element_type=jnp.float32)
+    part = (keep0 * jnp.dot(hidden1, down_weights, preferred_element_type=jnp.float32)
             - jnp.dot(hidden1, step0[2], preferred_element_type=jnp.float32))
     slopes1 = island_slopes(down(part), inputs[1], targets[1], hidden_units)
     slopes1 = slopes1.reshape(tokens, width)
-    hidden_slope = (keep0 * contract_last(slopes1, gathered[2])
+    hidden_slope = (keep0 * contract_last(slopes1, down_weights)
                     - contract_last(slopes1, step0[2])) * scale_out
     lhs1 = backward(slopes1, hidden1, hidden_slope, up_pre, activated, slope)
     rhs1 = jnp.stack([every[1], slopes1])

time: 449 us -> 356 us (0.79)
  waiting for transfers between devices: 106 us -> 0.04 us
  Pallas kernels: 243 us -> 284 us
  matrix products: 49.5 us -> 19.9 us
  local copies, waits for them, and re-layouts: 16.6 us -> 24.8 us
  other arithmetic: 8.92 us -> 2.95 us
    all_gather x1, waiting for transfers between devices: 106 us -> 0.02 us  [body(): lax.all_gather(weights[2].astype(jnp.bfloat16), 'isl', axis=1, tiled=True)]
    pallas_call x0 -> x1, Pallas kernels: none -> 41.4 us  [preactivations(): pl.pallas_call(preact_kernel, grid=(1,), out_shape=jax.ShapeDtypeStruct((...]
    dot_general x7 -> x3, matrix products: 36.1 us -> 9.4 us  [contract_last(): lax.dot_general(left_side, right_side, (((1,), (1,)), ((), ())), preferre...]
    convert_element_type x1, other arithmetic: 7.49 us -> 0.22 us  [body(): hidden1 = (activated * up_pre).astype(jnp.bfloat16)]
    unnamed x16 -> x36, local copies, waits for them, and re-layouts: 15.2 us -> 18.5 us
  transfers between devices with their start and end apart: 1 -> 1, of which waited for: 1 -> 0; matrix products, arithmetic and copies ran while one was open for 0% -> 2% of each run, Pallas kernels for 6% -> 19%
where the time goes in v2:
time: 356 us; the launch traced here: 353 us
  Pallas kernels  284 us (80%)
  local copies, waits for them, and re-layouts  24.8 us (7%)
  between operations  21 us (6%)
  matrix products  19.9 us (6%)
    pallas_call x1, Pallas kernels, last_update(): pl.pallas_call(functools.partial(last_kernel, chunks, per, tile, quarter,...  126 us
    pallas_call x2, Pallas kernels, island_slopes(): pl.pallas_call(functools.partial(slopes_kernel, n, 1.0 / math.sqrt(hidden...  55 us
    pallas_call x1, Pallas kernels, preactivations(): pl.pallas_call(preact_kernel, grid=(1,), out_shape=jax.ShapeDtypeStruct((...  41.4 us
    pallas_call x1, Pallas kernels, first_update(): pl.pallas_call(functools.partial(first_kernel, min(256, width)), grid=(ma...  36 us
    pallas_call x1, Pallas kernels, gather_inputs(): pl.pallas_call(functools.partial(gather_kernel, n, n_isl), out_shape=(jax...  25.3 us
    unnamed x36, local copies, waits for them, and re-layouts  18.5 us
    dot_general x3, matrix products, contract_last(): lax.dot_general(left_side, right_side, (((1,), (1,)), ((), ())), preferre...  9.4 us
  transfers between devices with their start and end apart: 1, of which 0 were waited for; matrix products, arithmetic and copies ran while one was open for 2% of the time, Pallas kernels for 19%

profile of v2, /device:TPU:0, one launch (start us, length us, event | category | flops | bytes accessed | tf_op | source)
XLA Modules:
  0.0 352.8 jit_solution(17336780572104859628)
XLA Ops:
  7.2 0.0 all-gather.3.cloned.1.call-start
  7.2 3.6 %slice.145 = bf16[1,896,1024]{2,1,0:T(8,128)(2,1)} slice(f32[3,896,1024]{2,1,0:T(8,128)} %w_ref.3), slice={[2:3], [0:896], [0:1024]} | slice | bytes 3670016 | tf_op jit(solution)/shard_map/slice | solution.py:459
  10.8 0.0 all-gather.3.cloned.1.call-update
  11.5 0.1 iota.7.flag_ref
  11.5 0.9 copy-done
  12.4 25.3 %gather_inputs.1 = (bf16[2,8,8,4096]{3,2,1,0:T(8,128)(2,1)S(1)}, f32[4,8,128]{2,1,0:T(8,128)S(1)}) custom-call(bf16[2,8,4096]{2,1,0:T(8,128)(2,1)S(1)} %copy-done, f32[8,128]{1,0:T(8,128)S(1)} %iota.7.flag_ref), custom_call_target="tpu_custom_call" | custom-call | tf_op jit(solution)/shard_map/gather_inputs/pallas_call | solution.py:87
  37.8 0.1 copy.36
  37.9 0.6 fusion.66
  43.8 0.1 pad.12.clone
  43.8 0.1 pad.13.clone
  43.9 0.7 multiply_bitcast_fusion
  44.6 0.1 copy.40
  44.7 0.7 multiply_bitcast_fusion.2
  45.3 0.1 copy.38
  45.4 0.1 copy.39
  45.5 0.1 copy.37
  45.6 0.8 reshape_reshape_reshape.3
  46.4 0.3 copy.57
  46.7 0.0 copy-start.10
  46.7 0.0 copy-start.11
  46.7 0.0 copy-start.1
  46.7 0.0 copy-start.9
  46.8 41.4 %preactivations.1 = f32[2,128,896]{2,1,0:T(8,128)S(1)} custom-call(bf16[4,128,1024]{2,1,0:T(8,128)(2,1)S(1)} %bitcast.221, f32[3,896,1024]{2,1,0:T(8,128)} %w_ref.3), custom_call_target="tpu_custom_call" | custom-call | tf_op jit(solution)/shard_map/preactivations/pallas_call | solution.py:166
  88.2 0.1 fusion.65
  88.3 1.0 copy.54
  89.3 0.2 copy.53
  89.5 0.0 copy-start.3
  89.5 0.2 copy.52
  89.7 0.0 copy-start.5
  89.7 1.0 copy.55
  90.7 0.6 fusion.64
  92.0 0.1 stack.77.coef_ref
  92.1 0.0 copy-done.10
  92.1 0.0 copy-done.11
  92.1 0.1 maximum_maximum_fusion.coef_ref
  92.2 0.2 fusion.49
  92.3 0.0 copy-done.3
  92.4 0.0 copy-done.5
  92.4 0.2 slice_bitcast_fusion.1
  92.6 0.0 copy-start.6
  92.6 0.0 all-gather.3.cloned.1.call-done
  92.7 0.0 copy-start.2
  92.7 4.6 %fusion.26.part_ref = bf16[8,8,4096]{2,1,0:T(8,128)(2,1)S(1)} fusion(bf16[64,896]{0,1:T(8,128)(2,1)S(1)} %fusion.49, bf16[1,896,4096]{2,1,0:T(8,128)(2,1)} %all-gather.3.cloned.1.call-done), kind=kOutput, calls=%fused_computation.18 | convolution fusion | flops 470024192 | bytes 7979008 | tf_op jit(solution)/shard_map/dot_general | solution.py:505
  97.3 25.8 %island_slopes.2 = bf16[8,8,4096]{2,1,0:T(8,128)(2,1)S(1)} custom-call(bf16[8,8,4096]{2,1,0:T(8,128)(2,1)S(1)} %fusion.26.part_ref, bf16[8,4096]{1,0:T(8,128)(2,1)S(1)} %get-tuple-element.31.x_ref, bf16[8,4096]{1,0:T(8,128)(2,1)S(1)} %get-tuple-element.22.y_ref), custom_call_target="tpu_custom_call" | custom-call | tf_op jit(solution)/shard_map/island_slopes/pallas_call | solution.py:225
  123.1 0.1 pad_maximum_fusion.rhs_ref.rhs0_ref
  123.3 2.1 fusion.61
  125.4 0.2 pad_maximum_fusion.2.lhs_ref.lhs0_ref
  125.6 36.0 %first_update.1 = (bf16[3,896,4096]{2,1,0:T(8,128)(2,1)}, f32[3,896,64]{2,1,0:T(8,128)S(1)}) custom-call(f32[3,4]{1,0:T(4,128)S(1)} %maximum_maximum_fusion.coef_ref, bf16[3,896,4096]{2,1,0:T(8,128)(2,1)} %bitcast.223, bf16[3,896,4096]{2,1,0:T(8,128)(2,1)} %bitcast.225, bf16[3,896,64]{2,1,0:T(8,128)(2,1)S(1)} %pad_maximum_fusion.2.lhs_ref.lhs0_ref, ...), custom_call_target="tpu_custom_call" | custom-call | tf_op jit(solution)/shard_map/first_update/pallas_call | solution.py:269
  161.6 0.0 copy-done.7
  161.6 0.2 multiply_convert_fusion.2
  161.8 1.4 fusion.17
  163.2 4.5 %fusion.29.part_ref = bf16[8,8,4096]{2,1,0:T(8,128)(2,1)S(1)} fusion(f32[64,4096]{1,0:T(8,128)S(1)} %fusion.17, bf16[64,896]{0,1:T(8,128)(2,1)S(1)} %multiply_convert_fusion.2, bf16[3,896,4096]{2,1,0:T(8,128)(2,1)} %get-tuple-element.8.p_ref), kind=kOutput, calls=%fused_computation.19 | convolution fusion | flops 470286336 | bytes 9027584 | tf_op jit(solution)/shard_map/dot_general | solution.py:518
  167.7 29.2 %island_slopes.3 = bf16[8,8,4096]{2,1,0:T(8,128)(2,1)S(1)} custom-call(bf16[8,8,4096]{2,1,0:T(8,128)(2,1)S(1)} %fusion.29.part_ref, bf16[8,4096]{1,0:T(8,128)(2,1)S(1)} %get-tuple-element.32.x_ref, bf16[8,4096]{1,0:T(8,128)(2,1)S(1)} %get-tuple-element.21.y_ref), custom_call_target="tpu_custom_call" | custom-call | tf_op jit(solution)/shard_map/island_slopes/pallas_call | solution.py:225
  196.9 2.0 fusion.35
  199.0 5.2 %fusion.60 = (bf16[1,896,64]{2,1,0:T(8,128)(2,1)S(1)}, bf16[1,896,64]{2,1,0:T(8,128)(2,1)S(1)}) fusion(f32[3,896,64]{2,1,0:T(8,128)S(1)} %get-tuple-element.9, f32[1,64,896]{1,2,0:T(8,128)S(1)} %copy-done.7, f32[]{:T(128)} %bitcast.35, f32[1,64,896]{1,2,0:T(8,128)S(1)} %copy-done.8, f32[64,896]{0,1:T(8,128)S(1)} %fusion.35, ...), kind=kOutput, calls=%fused_computation.61 | convolution fusion | flops 470966272 | bytes 9241088 | tf_op jit(solution)/shard_map/dot_general | solution.py:28
  204.2 0.1 pad_maximum_fusion.1.rhs1_ref
  204.3 0.2 pad_maximum_fusion.3.lhs1_ref
  204.5 126.3 %last_update.1 = (f32[3,896,1024]{2,1,0:T(8,128)}, f32[3,896,1024]{2,1,0:T(8,128)}) custom-call(f32[3,8]{1,0:T(4,128)S(1)} %stack.77.coef_ref, bf16[3,896,4096]{2,1,0:T(8,128)(2,1)} %bitcast.224, bf16[3,896,4096]{2,1,0:T(8,128)(2,1)} %bitcast.226, bf16[3,896,4096]{2,1,0:T(8,128)(2,1)} %get-tuple-element.8.p_ref, ...), custom_call_target="tpu_custom_call" | custom-call | tf_op jit(solution)/shard_map/last_update/pallas_call | solution.py:414
  330.7 0.0 slice-start
  330.8 0.0 slice-start.1
  330.8 0.0 slice-start.2
  330.8 10.9 %copy.61 = f32[3,896,1024]{2,1,0:T(8,128)} copy(f32[3,896,1024]{2,1,0:T(8,128)} %get-tuple-element.35) | data formatting | bytes 22020096
  341.7 0.0 slice-done.2
  341.7 4.3 %copy.62 = f32[3,896,1024]{2,1,0:T(8,128)} copy(f32[3,896,1024]{2,1,0:T(8,128)S(1)} %bitcast.228) | data formatting | bytes 22020096
  (20 shorter events, 0.1 us)
Async XLA Ops:
  7.2 85.5 %all-gather.3.cloned.1.call-start = ((), (), s32[]{:S(2)}) async-start(), calls=%async_computation | async-start | bytes 9175040 | tf_op jit(solution)/shard_map/all_gather | solution.py:459
  11.5 0.9 copy-start
  46.7 45.4 %copy-start.10 = (f32[3,1]{1,0:T(4,128)S(1)}, f32[3,1]{1,0:T(4,128)}, u32[]{:S(2)}) copy-start(f32[3,1]{1,0:T(4,128)} %constant.74) | copy-start | bytes 40
  46.7 45.4 %copy-start.11 = (f32[3,1]{1,0:T(4,128)S(1)}, f32[3,1]{1,0:T(4,128)}, u32[]{:S(2)}) copy-start(f32[3,1]{1,0:T(4,128)} %constant.72) | copy-start | bytes 40
  46.7 45.6 %copy-start.1 = (bf16[2,8,4096]{2,1,0:T(8,128)(2,1)S(1)}, bf16[2,8,4096]{2,1,0:T(8,128)(2,1)}, u32[]{:S(2)}) copy-start(bf16[2,8,4096]{2,1,0:T(8,128)(2,1)} %x_ref.1) | copy-start | bytes 393220
  46.7 45.6 %copy-start.9 = (bf16[2,8,4096]{2,1,0:T(8,128)(2,1)S(1)}, bf16[2,8,4096]{2,1,0:T(8,128)(2,1)}, u32[]{:S(2)}) copy-start(bf16[2,8,4096]{2,1,0:T(8,128)(2,1)} %param.13) | copy-start | bytes 393220
  89.5 2.9 copy-start.3
  89.7 2.7 copy-start.5
  92.6 30.6 %copy-start.4 = (f32[1,64,896]{1,2,0:T(8,128)S(1)}, f32[1,64,896]{1,2,0:T(8,128)}, u32[]{:S(2)}) copy-start(f32[1,64,896]{1,2,0:T(8,128)} %copy-done.3) | copy-start | bytes 688132
  92.6 30.6 %copy-start.6 = (f32[1,64,896]{1,2,0:T(8,128)S(1)}, f32[1,64,896]{1,2,0:T(8,128)}, u32[]{:S(2)}) copy-start(f32[1,64,896]{1,2,0:T(8,128)} %copy-done.5) | copy-start | bytes 688132
  92.7 30.6 %copy-start.2 = (bf16[1,896,4096]{2,1,0:T(8,128)(2,1)S(1)}, bf16[1,896,4096]{2,1,0:T(8,128)(2,1)}, u32[]{:S(2)}) copy-start(bf16[1,896,4096]{2,1,0:T(8,128)(2,1)} %all-gather.3.cloned.1.call-done) | copy-start | bytes 22020100
  125.6 36.0 %copy-start.7 = (f32[1,64,896]{1,2,0:T(8,128)S(1)}, f32[1,64,896]{1,2,0:T(8,128)}, u32[]{:S(2)}) copy-start(f32[1,64,896]{1,2,0:T(8,128)} %copy.54) | copy-start | bytes 688132
  125.6 36.0 %copy-start.8 = (f32[1,64,896]{1,2,0:T(8,128)S(1)}, f32[1,64,896]{1,2,0:T(8,128)}, u32[]{:S(2)}) copy-start(f32[1,64,896]{1,2,0:T(8,128)} %copy.55) | copy-start | bytes 688132
  330.7 10.9 %slice-start = ((s8[11010048]{0:T(1024)(128)(4,1)}), s8[4194304]{0:T(1024)(128)(4,1)S(1)}, s32[]{:S(2)}) async-start(s8[11010048]{0:T(1024)(128)(4,1)} %bitcast.227), calls=%async_computation.1 | async-start | bytes 8388608
  330.8 10.9 %slice-start.1 = ((s8[11010048]{0:T(1024)(128)(4,1)}), s8[4194304]{0:T(1024)(128)(4,1)S(1)}, s32[]{:S(2)}) async-start(s8[11010048]{0:T(1024)(128)(4,1)} %bitcast.227), calls=%async_computation.2 | async-start | bytes 8388608
  330.8 10.9 %slice-start.2 = ((s8[11010048]{0:T(1024)(128)(4,1)}), s8[2621440]{0:T(1024)(128)(4,1)S(1)}, s32[]{:S(2)}) async-start(s8[11010048]{0:T(1024)(128)(4,1)} %bitcast.227), calls=%async_computation.3 | async-start | bytes 5242880
Sparse Core Ops, SparseCore 0:
  10.9 66.4 all-gather.2

commit v3 on v2

--- a/solution.py
+++ b/solution.py
@@ -37,29 +37,66 @@
     pl.semaphore_wait(barrier, len(peers))
 
 
-def gather_kernel(n, n_isl, x_ref, flag_ref, out_ref, count_ref, got, flags, counts, own,
-                  send_sem, recv_sem, fsend_sem, frecv_sem, csend_sem, crecv_sem):
+def ring_of(me, n):
+    pair = me // 2 * 2 + lax.rem(me + 1, 2)
+    return pair, [lax.rem(me + 2 * d, n) for d in range(n // 2)]
+
+
+def spread(me, n, src, got_pair, got_ring, pair_send, pair_recv, ring_send, ring_recv):
+    pair, ring = ring_of(me, n)
+
+    def to_pair(block, d):
+        return pltpu.make_async_remote_copy(
+            block, got_pair.at[d], pair_send.at[d], pair_recv.at[d],
+            device_id={"fsdp": pair}, device_id_type=MESH)
+
+    def to_ring(d):
+        return pltpu.make_async_remote_copy(
+            src, got_ring.at[d - 1], ring_send.at[d - 1], ring_recv.at[d - 1],
+            device_id={"fsdp": ring[d]}, device_id_type=MESH)
+
+    around = [to_ring(d) for d in range(1, n // 2)]
+    for copy in around:
+        copy.start()
+    across = [to_pair(src, 0)]
+    across[0].start()
+
+    def arrivals():
+        for d in range(1, n // 2):
+            around[d - 1].wait_recv()
+            across.append(to_pair(got_ring.at[d - 1], d))
+            across[d].start()
+            yield lax.rem(me + n - 2 * d, n), got_ring.at[d - 1]
+        for d in range(n // 2):
+            across[d].wait_recv()
+            yield lax.rem(pair + n - 2 * d, n), got_pair.at[d]
+        for copy in around + across:
+            copy.wait_send()
+
+    return arrivals
+
+
+def gather_kernel(n, n_isl, x_ref, flag_ref, out_ref, count_ref, got_pair, got_ring, flags,
+                  counts, own, pair_send, pair_recv, ring_send, ring_recv,
+                  fsend_sem, frecv_sem, csend_sem, crecv_sem):
     isl = lax.axis_index("isl")
     me = lax.axis_index("fsdp")
     enter(
         [{"fsdp": lax.rem(me + d, n)} for d in range(1, n)]
         + [{"isl": lax.rem(isl + d, n_isl)} for d in range(1, n_isl)]
     )
-    copies = []
+    small = []
     for d in range(1, n):
-        to = {"fsdp": lax.rem(me + d, n)}
-        small = pltpu.make_async_remote_copy(
+        copy = pltpu.make_async_remote_copy(
             flag_ref, flags.at[d - 1], fsend_sem.at[d - 1], frecv_sem.at[d - 1],
-            device_id=to, device_id_type=MESH)
-        small.start()
-        big = pltpu.make_async_remote_copy(
-            x_ref, got.at[d - 1], send_sem.at[d - 1], recv_sem.at[d - 1],
-            device_id=to, device_id_type=MESH)
-        big.start()
-        copies.append((small, big))
+            device_id={"fsdp": lax.rem(me + d, n)}, device_id_type=MESH)
+        copy.start()
+        small.append(copy)
+    arrivals = spread(me, n, x_ref, got_pair, got_ring, pair_send, pair_recv, ring_send,
+                      ring_recv)
     total = flag_ref[...]
     for d in range(1, n):
-        copies[d - 1][0].wait()
+        small[d - 1].wait()
         total = total + flags[d - 1]
     own[...] = total
     sent = []
@@ -72,10 +109,9 @@
     count_ref[0] = total
     for k in range(x_ref.shape[0]):
         out_ref[k, me] = x_ref[k]
-    for d in range(1, n):
-        copies[d - 1][1].wait()
+    for device, block in arrivals():
         for k in range(x_ref.shape[0]):
-            out_ref[k, lax.rem(me + n - d, n)] = got[d - 1, k]
+            out_ref[k, device] = block[k]
     for d in range(1, n_isl):
         sent[d - 1].wait()
         count_ref[d] = counts[d - 1]
@@ -91,12 +127,12 @@
         in_specs=[vmem, vmem],
         out_specs=(vmem, vmem),
         scratch_shapes=[
-            pltpu.VMEM((n - 1, steps, rows, width), x.dtype),
+            pltpu.VMEM((n // 2, steps, rows, width), x.dtype),
+            pltpu.VMEM((n // 2, steps, rows, width), x.dtype),
             pltpu.VMEM((n - 1, 8, 128), jnp.float32),
             pltpu.VMEM((n_isl - 1, 8, 128), jnp.float32),
             pltpu.VMEM((8, 128), jnp.float32),
-            pltpu.SemaphoreType.DMA((n - 1,)),
-            pltpu.SemaphoreType.DMA((n - 1,)),
+        ] + [pltpu.SemaphoreType.DMA((n // 2,))] * 4 + [
             pltpu.SemaphoreType.DMA((n - 1,)),
             pltpu.SemaphoreType.DMA((n - 1,)),
             pltpu.SemaphoreType.DMA((n_isl - 1,)),
@@ -188,35 +224,40 @@
     )(x, w)
 
 
-def slopes_kernel(n, scale, inverse, part_ref, x_ref, y_ref, out_ref, got, own, back,
-                  send_sem, recv_sem, send_two, recv_two):
+def slopes_kernel(n, scale, inverse, part_ref, x_ref, y_ref, out_ref, got_one, sums, got_two,
+                  own, got_pair, got_ring, one_send, one_recv, two_send, two_recv,
+                  pair_send, pair_recv, ring_send, ring_recv):
     me = lax.axis_index("fsdp")
-    enter([{"fsdp": lax.rem(me + d, n)} for d in range(1, n)])
-    copies = []
-    for d in range(1, n):
-        peer = lax.rem(me + d, n)
-        copy = pltpu.make_async_remote_copy(
-            part_ref.at[peer], got.at[d - 1], send_sem.at[d - 1], recv_sem.at[d - 1],
-            device_id={"fsdp": peer}, device_id_type=MESH)
-        copy.start()
-        copies.append(copy)
-    total = part_ref[me].astype(jnp.float32)
-    for d in range(1, n):
-        copies[d - 1].wait()
-        total = total + got[d - 1].astype(jnp.float32)
+    pair, ring = ring_of(me, n)
+    half = n // 2
+    enter([{"fsdp": pair}] + [{"fsdp": ring[d]} for d in range(1, half)])
+    across = {}
+    for d in list(range(1, half)) + [0]:
+        across[d] = pltpu.make_async_remote_copy(
+            part_ref.at[lax.rem(pair + 2 * d, n)], got_one.at[d], one_send.at[d],
+            one_recv.at[d], device_id={"fsdp": pair}, device_id_type=MESH)
+        across[d].start()
+    around = {}
+    for d in range(1, half):
+        across[d].wait()
+        sums[d - 1] = (part_ref[ring[d]].astype(jnp.float32)
+                       + got_one[d].astype(jnp.float32)).astype(sums.dtype)
+        around[d] = pltpu.make_async_remote_copy(
+            sums.at[d - 1], got_two.at[d - 1], two_send.at[d - 1], two_recv.at[d - 1],
+            device_id={"fsdp": ring[d]}, device_id_type=MESH)
+        around[d].start()
+    across[0].wait()
+    total = part_ref[me].astype(jnp.float32) + got_one[0].astype(jnp.float32)
+    for d in range(1, half):
+        around[d].wait()
+        total = total + got_two[d - 1].astype(jnp.float32)
     outputs = x_ref[...].astype(jnp.float32) + total * scale
     own[...] = ((outputs - y_ref[...].astype(jnp.float32)) * inverse).astype(jnp.bfloat16)
-    copies = []
-    for d in range(1, n):
-        copy = pltpu.make_async_remote_copy(
-            own, back.at[d - 1], send_two.at[d - 1], recv_two.at[d - 1],
-            device_id={"fsdp": lax.rem(me + d, n)}, device_id_type=MESH)
-        copy.start()
-        copies.append(copy)
+    arrivals = spread(me, n, own, got_pair, got_ring, pair_send, pair_recv, ring_send,
+                      ring_recv)
     out_ref[me] = own[...]
-    for d in range(1, n):
-        copies[d - 1].wait()
-        out_ref[lax.rem(me + n - d, n)] = back[d - 1]
+    for device, block in arrivals():
+        out_ref[device] = block[...]
 
 
 def island_slopes(part, x, y, hidden_units):
@@ -229,14 +270,13 @@
         in_specs=[vmem] * 3,
         out_specs=vmem,
         scratch_shapes=[
-            pltpu.VMEM((n - 1, rows, width), part.dtype),
+            pltpu.VMEM((n // 2, rows, width), part.dtype),
+            pltpu.VMEM((n // 2, rows, width), part.dtype),
+            pltpu.VMEM((n // 2, rows, width), part.dtype),
             pltpu.VMEM((rows, width), jnp.bfloat16),
-            pltpu.VMEM((n - 1, rows, width), jnp.bfloat16),
-            pltpu.SemaphoreType.DMA((n - 1,)),
-            pltpu.SemaphoreType.DMA((n - 1,)),
-            pltpu.SemaphoreType.DMA((n - 1,)),
-            pltpu.SemaphoreType.DMA((n - 1,)),
-        ],
+            pltpu.VMEM((n // 2, rows, width), jnp.bfloat16),
+            pltpu.VMEM((n // 2, rows, width), jnp.bfloat16),
+        ] + [pltpu.SemaphoreType.DMA((n // 2,))] * 8,
         compiler_params=pltpu.CompilerParams(
             collective_id=1, has_side_effects=True, vmem_limit_bytes=40 << 20),
         name="island_slopes",

time: 356 us -> 345 us (0.969)
  Pallas kernels: 284 us -> 275 us
    pallas_call x2, Pallas kernels: 55 us -> 47 us  [island_slopes(): pl.pallas_call(functools.partial(slopes_kernel, n, 1.0 / math.sqrt(hidden...]
where the time goes in v3:
time: 345 us; the launch traced here: 344 us
  Pallas kernels  275 us (80%)
  local copies, waits for them, and re-layouts  24.8 us (7%)
  between operations  21 us (6%)
  matrix products  19.9 us (6%)
    pallas_call x1, Pallas kernels, last_update(): pl.pallas_call(functools.partial(last_kernel, chunks, per, tile, quarter,...  126 us
    pallas_call x2, Pallas kernels, island_slopes(): pl.pallas_call(functools.partial(slopes_kernel, n, 1.0 / math.sqrt(hidden...  47 us
    pallas_call x1, Pallas kernels, preactivations(): pl.pallas_call(preact_kernel, grid=(1,), out_shape=jax.ShapeDtypeStruct((...  41.8 us
    pallas_call x1, Pallas kernels, first_update(): pl.pallas_call(functools.partial(first_kernel, min(256, width)), grid=(ma...  36 us
    pallas_call x1, Pallas kernels, gather_inputs(): pl.pallas_call(functools.partial(gather_kernel, n, n_isl), out_shape=(jax...  23.7 us
    unnamed x36, local copies, waits for them, and re-layouts  18.5 us
    dot_general x3, matrix products, contract_last(): lax.dot_general(left_side, right_side, (((1,), (1,)), ((), ())), preferre...  9.4 us
  transfers between devices with their start and end apart: 1, of which 0 were waited for; matrix products, arithmetic and copies ran while one was open for 2% of the time, Pallas kernels for 19%

profile of v3, /device:TPU:0, one launch (start us, length us, event | category | flops | bytes accessed | tf_op | source)
XLA Modules:
  0.0 343.5 jit_solution(17038336092909153570)
XLA Ops:
  7.2 0.0 all-gather.3.cloned.1.call-start
  7.2 3.6 %slice.145 = bf16[1,896,1024]{2,1,0:T(8,128)(2,1)} slice(f32[3,896,1024]{2,1,0:T(8,128)} %w_ref.3), slice={[2:3], [0:896], [0:1024]} | slice | bytes 3670016 | tf_op jit(solution)/shard_map/slice | solution.py:499
  10.8 0.0 all-gather.3.cloned.1.call-update
  11.5 0.1 iota.7.flag_ref
  11.5 0.9 copy-done
  12.4 23.7 %gather_inputs.1 = (bf16[2,8,8,4096]{3,2,1,0:T(8,128)(2,1)S(1)}, f32[4,8,128]{2,1,0:T(8,128)S(1)}) custom-call(bf16[2,8,4096]{2,1,0:T(8,128)(2,1)S(1)} %copy-done, f32[8,128]{1,0:T(8,128)S(1)} %iota.7.flag_ref), custom_call_target="tpu_custom_call" | custom-call | tf_op jit(solution)/shard_map/gather_inputs/pallas_call | solution.py:123
  36.1 0.1 copy.36
  36.2 0.6 fusion.66
  42.1 0.1 pad.12.clone
  42.2 0.1 pad.13.clone
  42.3 0.7 multiply_bitcast_fusion
  42.9 0.1 copy.40
  43.0 0.7 multiply_bitcast_fusion.2
  43.7 0.1 copy.38
  43.8 0.1 copy.39
  43.9 0.1 copy.37
  43.9 0.8 reshape_reshape_reshape.3
  44.7 0.3 copy.57
  45.1 0.0 copy-start.10
  45.1 0.0 copy-start.11
  45.1 0.0 copy-start.1
  45.1 0.0 copy-start.9
  45.1 41.8 %preactivations.1 = f32[2,128,896]{2,1,0:T(8,128)S(1)} custom-call(bf16[4,128,1024]{2,1,0:T(8,128)(2,1)S(1)} %bitcast.221, f32[3,896,1024]{2,1,0:T(8,128)} %w_ref.3), custom_call_target="tpu_custom_call" | custom-call | tf_op jit(solution)/shard_map/preactivations/pallas_call | solution.py:202
  86.9 0.1 fusion.65
  87.0 1.0 copy.54
  88.0 0.2 copy.53
  88.2 0.0 copy-start.3
  88.2 0.2 copy.52
  88.4 0.0 copy-start.5
  88.4 1.0 copy.55
  89.4 0.6 fusion.64
  90.7 0.1 stack.77.coef_ref
  90.8 0.0 copy-done.10
  90.8 0.1 maximum_maximum_fusion.coef_ref
  90.9 0.2 fusion.49
  91.1 0.2 slice_bitcast_fusion.1
  91.3 0.0 copy-start.4
  91.3 0.0 copy-start.6
  91.4 0.0 all-gather.3.cloned.1.call-done
  91.4 0.0 copy-start.2
  91.4 4.6 %fusion.26.part_ref = bf16[8,8,4096]{2,1,0:T(8,128)(2,1)S(1)} fusion(bf16[64,896]{0,1:T(8,128)(2,1)S(1)} %fusion.49, bf16[1,896,4096]{2,1,0:T(8,128)(2,1)} %all-gather.3.cloned.1.call-done), kind=kOutput, calls=%fused_computation.18 | convolution fusion | flops 470024192 | bytes 7979008 | tf_op jit(solution)/shard_map/dot_general | solution.py:545
  96.0 24.8 %island_slopes.2 = bf16[8,8,4096]{2,1,0:T(8,128)(2,1)S(1)} custom-call(bf16[8,8,4096]{2,1,0:T(8,128)(2,1)S(1)} %fusion.26.part_ref, bf16[8,4096]{1,0:T(8,128)(2,1)S(1)} %get-tuple-element.31.x_ref, bf16[8,4096]{1,0:T(8,128)(2,1)S(1)} %get-tuple-element.22.y_ref), custom_call_target="tpu_custom_call" | custom-call | tf_op jit(solution)/shard_map/island_slopes/pallas_call | solution.py:266
  120.8 0.1 pad_maximum_fusion.rhs_ref.rhs0_ref
  121.0 2.1 fusion.61
  123.1 0.2 pad_maximum_fusion.2.lhs_ref.lhs0_ref
  123.3 0.0 copy-start.7
  123.3 0.0 copy-start.8
  123.3 36.0 %first_update.1 = (bf16[3,896,4096]{2,1,0:T(8,128)(2,1)}, f32[3,896,64]{2,1,0:T(8,128)S(1)}) custom-call(f32[3,4]{1,0:T(4,128)S(1)} %maximum_maximum_fusion.coef_ref, bf16[3,896,4096]{2,1,0:T(8,128)(2,1)} %bitcast.223, bf16[3,896,4096]{2,1,0:T(8,128)(2,1)} %bitcast.225, bf16[3,896,64]{2,1,0:T(8,128)(2,1)S(1)} %pad_maximum_fusion.2.lhs_ref.lhs0_ref, ...), custom_call_target="tpu_custom_call" | custom-call | tf_op jit(solution)/shard_map/first_update/pallas_call | solution.py:309
  159.3 0.0 copy-done.7
  159.3 0.2 multiply_convert_fusion.2
  159.5 1.4 fusion.17
  160.9 4.5 %fusion.29.part_ref = bf16[8,8,4096]{2,1,0:T(8,128)(2,1)S(1)} fusion(f32[64,4096]{1,0:T(8,128)S(1)} %fusion.17, bf16[64,896]{0,1:T(8,128)(2,1)S(1)} %multiply_convert_fusion.2, bf16[3,896,4096]{2,1,0:T(8,128)(2,1)} %get-tuple-element.8.p_ref), kind=kOutput, calls=%fused_computation.19 | convolution fusion | flops 470286336 | bytes 9027584 | tf_op jit(solution)/shard_map/dot_general | solution.py:558
  165.4 22.3 %island_slopes.3 = bf16[8,8,4096]{2,1,0:T(8,128)(2,1)S(1)} custom-call(bf16[8,8,4096]{2,1,0:T(8,128)(2,1)S(1)} %fusion.29.part_ref, bf16[8,4096]{1,0:T(8,128)(2,1)S(1)} %get-tuple-element.32.x_ref, bf16[8,4096]{1,0:T(8,128)(2,1)S(1)} %get-tuple-element.21.y_ref), custom_call_target="tpu_custom_call" | custom-call | tf_op jit(solution)/shard_map/island_slopes/pallas_call | solution.py:266
  187.7 2.0 fusion.35
  189.7 5.2 %fusion.60 = (bf16[1,896,64]{2,1,0:T(8,128)(2,1)S(1)}, bf16[1,896,64]{2,1,0:T(8,128)(2,1)S(1)}) fusion(f32[3,896,64]{2,1,0:T(8,128)S(1)} %get-tuple-element.9, f32[1,64,896]{1,2,0:T(8,128)S(1)} %copy-done.7, f32[]{:T(128)} %bitcast.35, f32[1,64,896]{1,2,0:T(8,128)S(1)} %copy-done.8, f32[64,896]{0,1:T(8,128)S(1)} %fusion.35, ...), kind=kOutput, calls=%fused_computation.61 | convolution fusion | flops 470966272 | bytes 9241088 | tf_op jit(solution)/shard_map/dot_general | solution.py:28
  195.0 0.1 pad_maximum_fusion.1.rhs1_ref
  195.1 0.2 pad_maximum_fusion.3.lhs1_ref
  195.3 126.3 %last_update.1 = (f32[3,896,1024]{2,1,0:T(8,128)}, f32[3,896,1024]{2,1,0:T(8,128)}) custom-call(f32[3,8]{1,0:T(4,128)S(1)} %stack.77.coef_ref, bf16[3,896,4096]{2,1,0:T(8,128)(2,1)} %bitcast.224, bf16[3,896,4096]{2,1,0:T(8,128)(2,1)} %bitcast.226, bf16[3,896,4096]{2,1,0:T(8,128)(2,1)} %get-tuple-element.8.p_ref, ...), custom_call_target="tpu_custom_call" | custom-call | tf_op jit(solution)/shard_map/last_update/pallas_call | solution.py:454
  321.5 0.0 slice-start
  321.5 0.0 slice-start.1
  321.5 0.0 slice-start.2
  321.5 10.9 %copy.61 = f32[3,896,1024]{2,1,0:T(8,128)} copy(f32[3,896,1024]{2,1,0:T(8,128)} %get-tuple-element.35) | data formatting | bytes 22020096
  332.4 0.0 slice-done
  332.4 4.3 %copy.62 = f32[3,896,1024]{2,1,0:T(8,128)} copy(f32[3,896,1024]{2,1,0:T(8,128)S(1)} %bitcast.228) | data formatting | bytes 22020096
  (20 shorter events, 0.1 us)
Async XLA Ops:
  7.2 84.2 %all-gather.3.cloned.1.call-start = ((), (), s32[]{:S(2)}) async-start(), calls=%async_computation | async-start | bytes 9175040 | tf_op jit(solution)/shard_map/all_gather | solution.py:499
  11.5 0.9 copy-start
  45.1 45.8 %copy-start.10 = (f32[3,1]{1,0:T(4,128)S(1)}, f32[3,1]{1,0:T(4,128)}, u32[]{:S(2)}) copy-start(f32[3,1]{1,0:T(4,128)} %constant.74) | copy-start | bytes 40
  45.1 45.8 %copy-start.11 = (f32[3,1]{1,0:T(4,128)S(1)}, f32[3,1]{1,0:T(4,128)}, u32[]{:S(2)}) copy-start(f32[3,1]{1,0:T(4,128)} %constant.72) | copy-start | bytes 40
  45.1 46.0 %copy-start.1 = (bf16[2,8,4096]{2,1,0:T(8,128)(2,1)S(1)}, bf16[2,8,4096]{2,1,0:T(8,128)(2,1)}, u32[]{:S(2)}) copy-start(bf16[2,8,4096]{2,1,0:T(8,128)(2,1)} %x_ref.1) | copy-start | bytes 393220
  45.1 46.0 %copy-start.9 = (bf16[2,8,4096]{2,1,0:T(8,128)(2,1)S(1)}, bf16[2,8,4096]{2,1,0:T(8,128)(2,1)}, u32[]{:S(2)}) copy-start(bf16[2,8,4096]{2,1,0:T(8,128)(2,1)} %param.13) | copy-start | bytes 393220
  88.2 2.9 copy-start.3
  88.4 2.7 copy-start.5
  91.3 29.6 %copy-start.4 = (f32[1,64,896]{1,2,0:T(8,128)S(1)}, f32[1,64,896]{1,2,0:T(8,128)}, u32[]{:S(2)}) copy-start(f32[1,64,896]{1,2,0:T(8,128)} %copy-done.3) | copy-start | bytes 688132
  91.3 29.6 %copy-start.6 = (f32[1,64,896]{1,2,0:T(8,128)S(1)}, f32[1,64,896]{1,2,0:T(8,128)}, u32[]{:S(2)}) copy-start(f32[1,64,896]{1,2,0:T(8,128)} %copy-done.5) | copy-start | bytes 688132
  91.4 29.6 %copy-start.2 = (bf16[1,896,4096]{2,1,0:T(8,128)(2,1)S(1)}, bf16[1,896,4096]{2,1,0:T(8,128)(2,1)}, u32[]{:S(2)}) copy-start(bf16[1,896,4096]{2,1,0:T(8,128)(2,1)} %all-gather.3.cloned.1.call-done) | copy-start | bytes 22020100
  123.3 36.0 %copy-start.7 = (f32[1,64,896]{1,2,0:T(8,128)S(1)}, f32[1,64,896]{1,2,0:T(8,128)}, u32[]{:S(2)}) copy-start(f32[1,64,896]{1,2,0:T(8,128)} %copy.54) | copy-start | bytes 688132
  123.3 36.0 %copy-start.8 = (f32[1,64,896]{1,2,0:T(8,128)S(1)}, f32[1,64,896]{1,2,0:T(8,128)}, u32[]{:S(2)}) copy-start(f32[1,64,896]{1,2,0:T(8,128)} %copy.55) | copy-start | bytes 688132
  321.5 10.9 %slice-start = ((s8[11010048]{0:T(1024)(128)(4,1)}), s8[4194304]{0:T(1024)(128)(4,1)S(1)}, s32[]{:S(2)}) async-start(s8[11010048]{0:T(1024)(128)(4,1)} %bitcast.227), calls=%async_computation.1 | async-start | bytes 8388608
  321.5 10.9 %slice-start.1 = ((s8[11010048]{0:T(1024)(128)(4,1)}), s8[4194304]{0:T(1024)(128)(4,1)S(1)}, s32[]{:S(2)}) async-start(s8[11010048]{0:T(1024)(128)(4,1)} %bitcast.227), calls=%async_computation.2 | async-start | bytes 8388608
  321.5 10.9 %slice-start.2 = ((s8[11010048]{0:T(1024)(128)(4,1)}), s8[2621440]{0:T(1024)(128)(4,1)S(1)}, s32[]{:S(2)}) async-start(s8[11010048]{0:T(1024)(128)(4,1)} %bitcast.227), calls=%async_computation.3 | async-start | bytes 5242880
Sparse Core Ops, SparseCore 0:
  10.9 66.3 all-gather.2
